TPU v7x, 32 devices: a whole 2x2x4 slice. The times are simulated.
32 devices in a mesh: dp: 4 (over y, x), seq: 8 (over z, core).
Axes of the slice: x: 2, y: 2, z: 4, core: 2. Of those that a mesh axis runs over, the one named last changes fastest.
Arguments:
- inputs: bfloat16 [8, 1024, 1024], P('dp', 'seq'), may hold values from -6 to 6
- cotangent: bfloat16 [8, 1024, 1024], P('dp', 'seq'), may hold values from -6 to 6
- lengths: int32 [8], P('dp'), may hold values from 256 to 1024, as said below
- block_order: int32 [16], replicated, may hold values from 0 to 15, each once
- step_count: int32 [], replicated, may hold values from 2 to 20
- learn_rates: float32 [6], replicated, as said below
- w_qkv: float32 [1024, 3072], P(('dp', 'seq')), may hold values from -0.1875 to 0.1875
- w_proj: float32 [1024, 1024], P(('dp', 'seq')), may hold values from -1.5 to 1.5
- w_expand: float32 [1024, 4096], P(('dp', 'seq')), may hold values from -0.1875 to 0.1875
- w_shrink: float32 [4096, 1024], P(('dp', 'seq')), may hold values from -0.09375 to 0.09375
- vectors: float32 [1024, 8], P(('dp', 'seq')), as said below
- bias_expand: float32 [4096], P(('dp', 'seq')), may hold values from -1 to 1
- first_qkv: float32 [1024, 3072], P(('dp', 'seq')), may hold values from -0.00018310547 to 0.00018310547
- first_proj: float32 [1024, 1024], P(('dp', 'seq')), may hold values from -0.00018310547 to 0.00018310547
- first_expand: float32 [1024, 4096], P(('dp', 'seq')), may hold values from -0.00018310547 to 0.00018310547
- first_shrink: float32 [4096, 1024], P(('dp', 'seq')), may hold values from -0.00018310547 to 0.00018310547
- first_vectors: float32 [1024, 8], P(('dp', 'seq')), may hold values from -0.00018310547 to 0.00018310547
- first_bias: float32 [4096], P(('dp', 'seq')), may hold values from -0.00018310547 to 0.00018310547
- second_qkv: float32 [1024, 3072], P(('dp', 'seq')), may hold values from 4.207952e-09 to 1.6673019e-08
- second_proj: float32 [1024, 1024], P(('dp', 'seq')), may hold values from 4.207952e-09 to 1.6673019e-08
- second_expand: float32 [1024, 4096], P(('dp', 'seq')), may hold values from 4.207952e-09 to 1.6673019e-08
- second_shrink: float32 [4096, 1024], P(('dp', 'seq')), may hold values from 4.207952e-09 to 1.6673019e-08
- second_vectors: float32 [1024, 8], P(('dp', 'seq')), may hold values from 4.207952e-09 to 1.6673019e-08
- second_bias: float32 [4096], P(('dp', 'seq')), may hold values from 4.207952e-09 to 1.6673019e-08
Outputs:
- layer_out: float32 [8, 1024, 1024], P('dp', 'seq')
- grad_inputs: float32 [8, 1024, 1024], P('dp', 'seq')
- grad_norm: float32 [], replicated
- new_qkv: float32 [1024, 3072], P(('dp', 'seq'))
- new_proj: float32 [1024, 1024], P(('dp', 'seq'))
- new_expand: float32 [1024, 4096], P(('dp', 'seq'))
- new_shrink: float32 [4096, 1024], P(('dp', 'seq'))
- new_vectors: float32 [1024, 8], P(('dp', 'seq'))
- new_bias: float32 [4096], P(('dp', 'seq'))
- new_first_qkv: float32 [1024, 3072], P(('dp', 'seq'))
- new_first_proj: float32 [1024, 1024], P(('dp', 'seq'))
- new_first_expand: float32 [1024, 4096], P(('dp', 'seq'))
- new_first_shrink: float32 [4096, 1024], P(('dp', 'seq'))
- new_first_vectors: float32 [1024, 8], P(('dp', 'seq'))
- new_first_bias: float32 [4096], P(('dp', 'seq'))
- new_second_qkv: float32 [1024, 3072], P(('dp', 'seq'))
- new_second_proj: float32 [1024, 1024], P(('dp', 'seq'))
- new_second_expand: float32 [1024, 4096], P(('dp', 'seq'))
- new_second_shrink: float32 [4096, 1024], P(('dp', 'seq'))
- new_second_vectors: float32 [1024, 8], P(('dp', 'seq'))
- new_second_bias: float32 [4096], P(('dp', 'seq'))
Inputs may be any that keep to these rules, and one draw needn't show every extreme that they name: `lengths`: slots from a sequence's length on are padding; some sequence is full and some has exactly 256 valid slots. A permutation: block b of 64 slots of every sequence holds positions block_order[b] * 64 onward. `learn_rates`: positive rates in the order w_qkv, w_proj, w_expand, w_shrink, vectors, bias_expand. `vectors`: columns 0 and 5 are gains near one, the other columns biases.
All inputs are finite; a program needn't handle non-finite values.
Results may differ from a plain program's by a relative error of at most 0.009.
The roundings to bfloat16 on the way count: a program that leaves them out, or rounds other values in their place, can miss the bound.
Values may be sent and summed in bfloat16 or wider, within the bound.
A program may use at most 104 MiB of HBM per device.

v0:
```python
import math

import jax
import jax.numpy as jnp
from jax import lax
from jax.sharding import PartitionSpec as P

HEADS = 16
HD = 64


norm_eps = 1e-05
neg_fill = -1e30
beta_first = 0.9
beta_second = 0.95
adam_eps = 1e-08
decay_rate = 0.1
clip_bound = 1.0


def layer_norm(values, gain_vec, shift_vec):
    centered = values - jnp.mean(values, axis=-1, keepdims=True)
    variance = jnp.mean(centered * centered, axis=-1, keepdims=True)
    return centered * lax.rsqrt(variance + norm_eps) * gain_vec + shift_vec


def slot_positions(slot_ids, order_table, block_len):
    block_ids = jnp.arange(order_table.shape[0], dtype=jnp.int32)
    one_hot = (slot_ids[:, None] // block_len == block_ids[None, :]).astype(jnp.int32)
    picked = jnp.sum(one_hot * order_table[None, :], axis=1)
    return picked * block_len + slot_ids % block_len


def contract_rows(left, right):
    return lax.dot_general(
        left, right, (((0,), (0,)), ((), ())), preferred_element_type=jnp.float32
    )


def contract_cols(left, right):
    return lax.dot_general(
        left, right, (((1,), (1,)), ((), ())), preferred_element_type=jnp.float32
    )


def masked_scores(queries, key_block, query_pos, key_pos, length, score_scale):
    scores = (
        jnp.einsum("qhd,khd->hqk", queries, key_block, preferred_element_type=jnp.float32)
        * score_scale
    )
    allowed = (key_pos[None, :] <= query_pos[:, None]) & (key_pos[None, :] < length)
    return jnp.where(allowed[None], scores, neg_fill)


def softmax_rows(queries, key_block, query_pos, key_pos, length, score_scale):
    scores = masked_scores(queries, key_block, query_pos, key_pos, length, score_scale)
    row_max = jnp.max(scores, axis=-1, keepdims=True)
    exp_scores = jnp.exp(scores - row_max)
    row_total = jnp.sum(exp_scores, axis=-1, keepdims=True)
    return (exp_scores / row_total, row_max + jnp.log(row_total))


def per_device(
    inputs,
    cotangent,
    lengths,
    block_order,
    step_count,
    learn_rates,
    w_qkv,
    w_proj,
    w_expand,
    w_shrink,
    vectors,
    bias_expand,
    first_qkv,
    first_proj,
    first_expand,
    first_shrink,
    first_vectors,
    first_bias,
    second_qkv,
    second_proj,
    second_expand,
    second_shrink,
    second_vectors,
    second_bias,
):
    low_type = jnp.bfloat16
    wide_type = jnp.float32
    seqs_here, local_slots, model_width = inputs.shape
    total_slots = local_slots * lax.axis_size("seq")
    block_len = total_slots // block_order.shape[0]
    score_scale = 1.0 / math.sqrt(HD)
    token_count = seqs_here * local_slots
    first_slot = lax.axis_index("seq") * local_slots
    local_pos = slot_positions(
        first_slot + jnp.arange(local_slots, dtype=jnp.int32), block_order, block_len
    )
    key_pos = slot_positions(jnp.arange(total_slots, dtype=jnp.int32), block_order, block_len)
    valid_rows = (local_pos[None, :] < lengths[:, None]).astype(wide_type)
    rows_in = inputs.reshape(token_count, model_width).astype(wide_type)
    qkv_full, proj_full, vec_full = (
        lax.all_gather(w_qkv.astype(low_type), ("dp", "seq"), axis=0, tiled=True),
        lax.all_gather(w_proj.astype(low_type), ("dp", "seq"), axis=0, tiled=True),
        lax.all_gather(vectors.astype(low_type), ("dp", "seq"), axis=0, tiled=True),
    )
    vec_wide = vec_full.astype(wide_type)
    gain_one = vec_wide[:, 0]
    shift_one = vec_wide[:, 1]
    bias_query = vec_wide[:, 2]
    bias_value = vec_wide[:, 3]
    bias_proj = vec_wide[:, 4]
    gain_two = vec_wide[:, 5]
    shift_two = vec_wide[:, 6]
    bias_shrink = vec_wide[:, 7]
    normed_one = layer_norm(rows_in, gain_one, shift_one).astype(low_type)
    bias_cat = jnp.concatenate([bias_query, jnp.zeros_like(bias_query), bias_value])
    qkv_rows = (jnp.dot(normed_one, qkv_full, preferred_element_type=wide_type) + bias_cat).astype(
        low_type
    )
    head_shape = (seqs_here, local_slots, HEADS, HD)
    query_all = qkv_rows[:, :model_width].reshape(head_shape)
    key_local = qkv_rows[:, model_width : 2 * model_width].reshape(head_shape)
    value_local = qkv_rows[:, 2 * model_width :].reshape(head_shape)
    keys_all, values_all = (
        lax.all_gather(key_local, "seq", axis=1, tiled=True),
        lax.all_gather(value_local, "seq", axis=1, tiled=True),
    )

    def forward_one(packed):
        queries, key_block, value_block, length = packed
        softmax_w, row_lse = softmax_rows(
            queries, key_block, local_pos, key_pos, length, score_scale
        )
        return jnp.einsum(
            "hqk,khd->qhd",
            softmax_w.astype(low_type),
            value_block,
            preferred_element_type=wide_type,
        )

    context = lax.map(forward_one, (query_all, keys_all, values_all, lengths))
    context_low = context.reshape(token_count, model_width).astype(low_type)
    attn_rows = jnp.dot(context_low, proj_full, preferred_element_type=wide_type) + bias_proj
    resid = rows_in + attn_rows
    expand_full, shrink_full, bias_full = (
        lax.all_gather(w_expand.astype(low_type), ("dp", "seq"), axis=0, tiled=True),
        lax.all_gather(w_shrink.astype(low_type), ("dp", "seq"), axis=0, tiled=True),
        lax.all_gather(bias_expand.astype(low_type), ("dp", "seq"), axis=0, tiled=True),
    )
    normed_two = layer_norm(resid, gain_two, shift_two).astype(low_type)
    pre_act = jnp.dot(normed_two, expand_full, preferred_element_type=wide_type) + bias_full.astype(
        wide_type
    )
    gelu_out, gelu_back = jax.vjp(lambda arg_in: jax.nn.gelu(arg_in, approximate=True), pre_act)
    act_low = gelu_out.astype(low_type)
    layer_rows = (
        resid + jnp.dot(act_low, shrink_full, preferred_element_type=wide_type) + bias_shrink
    )
    grad_rows = (cotangent.astype(wide_type) * valid_rows[:, :, None]).reshape(
        token_count, model_width
    )
    grad_low = grad_rows.astype(low_type)
    grad_shrink = contract_rows(act_low, grad_low)
    grad_bias_shrink = jnp.sum(grad_rows, axis=0)
    expand_back, shrink_back = (
        lax.all_gather(w_expand.astype(low_type), ("dp", "seq"), axis=0, tiled=True),
        lax.all_gather(w_shrink.astype(low_type), ("dp", "seq"), axis=0, tiled=True),
    )
    grad_act = contract_cols(grad_low, shrink_back)
    grad_pre = gelu_back(grad_act)[0].astype(low_type)
    grad_expand = contract_rows(normed_two, grad_pre)
    grad_bias_expand = jnp.sum(grad_pre, axis=0, dtype=wide_type)
    grad_normed_two = contract_cols(grad_pre, expand_back)
    norm_two_out, norm_back_two = jax.vjp(layer_norm, resid, gain_two, shift_two)
    grad_resid_part, grad_gain_two, grad_shift_two = norm_back_two(grad_normed_two)
    grad_resid = grad_rows + grad_resid_part
    grad_expand_mine, grad_shrink_mine, grad_bias_mine = (
        lax.psum_scatter(grad_expand, ("dp", "seq"), scatter_dimension=0, tiled=True),
        lax.psum_scatter(grad_shrink, ("dp", "seq"), scatter_dimension=0, tiled=True),
        lax.psum_scatter(grad_bias_expand, ("dp", "seq"), scatter_dimension=0, tiled=True),
    )
    grad_attn_low = grad_resid.astype(low_type)
    grad_proj = contract_rows(context_low, grad_attn_low)
    grad_bias_proj = jnp.sum(grad_attn_low, axis=0, dtype=wide_type)
    qkv_back, proj_back = (
        lax.all_gather(w_qkv.astype(low_type), ("dp", "seq"), axis=0, tiled=True),
        lax.all_gather(w_proj.astype(low_type), ("dp", "seq"), axis=0, tiled=True),
    )
    grad_context = contract_cols(grad_attn_low, proj_back).astype(low_type).reshape(head_shape)
    keys_back, values_back = (
        lax.all_gather(key_local, "seq", axis=1, tiled=True),
        lax.all_gather(value_local, "seq", axis=1, tiled=True),
    )

    def backward_one(packed):
        queries, key_block, value_block, grad_ctx, length = packed
        softmax_w, row_lse = softmax_rows(
            queries, key_block, local_pos, key_pos, length, score_scale
        )
        grad_prob = jnp.einsum(
            "qhd,khd->hqk", grad_ctx, value_block, preferred_element_type=wide_type
        )
        delta = jnp.sum(softmax_w * grad_prob, axis=-1, keepdims=True)
        grad_score = (softmax_w * (grad_prob - delta)).astype(low_type)
        grad_query = (
            jnp.einsum("hqk,khd->qhd", grad_score, key_block, preferred_element_type=wide_type)
            * score_scale
        )
        key_terms = (
            jnp.einsum("hqk,qhd->khd", grad_score, queries, preferred_element_type=wide_type)
            * score_scale
        )
        value_terms = jnp.einsum(
            "hqk,qhd->khd", softmax_w.astype(low_type), grad_ctx, preferred_element_type=wide_type
        )
        return (grad_query, key_terms, value_terms)

    grad_query, key_terms, value_terms = lax.map(
        backward_one, (query_all, keys_back, values_back, grad_context, lengths)
    )
    key_sums, value_sums = (
        lax.psum_scatter(key_terms, "seq", scatter_dimension=1, tiled=True),
        lax.psum_scatter(value_terms, "seq", scatter_dimension=1, tiled=True),
    )
    grad_q_low = grad_query.reshape(token_count, model_width).astype(low_type)
    grad_v_low = value_sums.reshape(token_count, model_width).astype(low_type)
    grad_qkv_rows = jnp.concatenate(
        [grad_q_low, key_sums.reshape(token_count, model_width).astype(low_type), grad_v_low],
        axis=1,
    )
    grad_qkv_w = contract_rows(normed_one, grad_qkv_rows)
    grad_bias_query = jnp.sum(grad_q_low, axis=0, dtype=wide_type)
    grad_bias_value = jnp.sum(grad_v_low, axis=0, dtype=wide_type)
    grad_normed_one = contract_cols(grad_qkv_rows, qkv_back)
    norm_one_out, norm_back_one = jax.vjp(layer_norm, rows_in, gain_one, shift_one)
    grad_in_part, grad_gain_one, grad_shift_one = norm_back_one(grad_normed_one)
    grad_in_rows = grad_resid + grad_in_part
    grad_vec = jnp.stack(
        [
            grad_gain_one,
            grad_shift_one,
            grad_bias_query,
            grad_bias_value,
            grad_bias_proj,
            grad_gain_two,
            grad_shift_two,
            grad_bias_shrink,
        ],
        axis=1,
    )
    grad_qkv_mine, grad_proj_mine, grad_vec_mine = (
        lax.psum_scatter(grad_qkv_w, ("dp", "seq"), scatter_dimension=0, tiled=True),
        lax.psum_scatter(grad_proj, ("dp", "seq"), scatter_dimension=0, tiled=True),
        lax.psum_scatter(grad_vec, ("dp", "seq"), scatter_dimension=0, tiled=True),
    )
    grads = (
        grad_qkv_mine,
        grad_proj_mine,
        grad_expand_mine,
        grad_shrink_mine,
        grad_vec_mine,
        grad_bias_mine,
    )
    masters = (w_qkv, w_proj, w_expand, w_shrink, vectors, bias_expand)
    firsts = (first_qkv, first_proj, first_expand, first_shrink, first_vectors, first_bias)
    seconds = (second_qkv, second_proj, second_expand, second_shrink, second_vectors, second_bias)
    square_sum = sum((jnp.sum(gradient * gradient) for gradient in grads))
    total_square = lax.psum(square_sum, ("dp", "seq"))
    grad_norm = jnp.sqrt(total_square)
    clip_factor = clip_bound / jnp.maximum(grad_norm, clip_bound)
    step_float = step_count.astype(wide_type)
    correct_first = 1.0 - beta_first**step_float
    correct_second = 1.0 - beta_second**step_float
    renewed = []
    first_new = []
    second_new = []
    for group_id in range(6):
        clipped = grads[group_id] * clip_factor
        moment_one = beta_first * firsts[group_id] + (1.0 - beta_first) * clipped
        moment_two = beta_second * seconds[group_id] + (1.0 - beta_second) * clipped * clipped
        update = moment_one / correct_first / (jnp.sqrt(moment_two / correct_second) + adam_eps)
        if group_id < 4:
            update = update + decay_rate * masters[group_id]
        renewed.append(masters[group_id] - learn_rates[group_id] * update)
        first_new.append(moment_one)
        second_new.append(moment_two)
    layer_out = layer_rows.reshape(seqs_here, local_slots, model_width)
    grad_inputs = grad_in_rows.reshape(seqs_here, local_slots, model_width)
    return (
        (layer_out, grad_inputs, grad_norm) + tuple(renewed) + tuple(first_new) + tuple(second_new)
    )


def solution(mesh):
    return jax.shard_map(
        per_device,
        mesh=mesh,
        in_specs=(
            P("dp", "seq", None),
            P("dp", "seq", None),
            P("dp"),
            P(),
            P(),
            P(),
            P(("dp", "seq"), None),
            P(("dp", "seq"), None),
            P(("dp", "seq"), None),
            P(("dp", "seq"), None),
            P(("dp", "seq"), None),
            P(("dp", "seq")),
            P(("dp", "seq"), None),
            P(("dp", "seq"), None),
            P(("dp", "seq"), None),
            P(("dp", "seq"), None),
            P(("dp", "seq"), None),
            P(("dp", "seq")),
            P(("dp", "seq"), None),
            P(("dp", "seq"), None),
            P(("dp", "seq"), None),
            P(("dp", "seq"), None),
            P(("dp", "seq"), None),
            P(("dp", "seq")),
        ),
        out_specs=(
            P("dp", "seq", None),
            P("dp", "seq", None),
            P(),
            P(("dp", "seq"), None),
            P(("dp", "seq"), None),
            P(("dp", "seq"), None),
            P(("dp", "seq"), None),
            P(("dp", "seq"), None),
            P(("dp", "seq")),
            P(("dp", "seq"), None),
            P(("dp", "seq"), None),
            P(("dp", "seq"), None),
            P(("dp", "seq"), None),
            P(("dp", "seq"), None),
            P(("dp", "seq")),
            P(("dp", "seq"), None),
            P(("dp", "seq"), None),
            P(("dp", "seq"), None),
            P(("dp", "seq"), None),
            P(("dp", "seq"), None),
            P(("dp", "seq")),
        ),
        check_vma=False,
    )
```

profile of v0, /device:TPU:0, one launch (start us, length us, event | category | flops | bytes accessed | tf_op | source)
XLA Modules:
  0.0 1530.8 jit_solution(9304684250127424476)
XLA Ops:
  11.6 43.8 %all-gather = bf16[32,32,8]{1,2,0:T(8,128)(2,1)S(1)} all-gather(bf16[1,32,8]{1,2,0:T(8,128)(2,1)S(1)} %convert_bitcast_fusion), channel_id=1, replica_groups=mesh['dp'=4,'seq'=8] {'dp','seq'}, dimensions={0}, use_global_device_ids=true | all-gather | bytes 16896 | tf_op jit(solution)/shard_map/all_gather | solution.py:106
  60.1 23.8 %all-gather.9.cloned.1.call-done = bf16[1024,3072]{1,0:T(8,128)(2,1)} async-done(((bf16[32,3072]{1,0:T(8,128)(2,1)}), bf16[1024,3072]{1,0:T(8,128)(2,1)}) %all-gather.9.cloned.1.call-update) | async-done | bytes 6291472 | tf_op jit(solution)/shard_map/all_gather | solution.py:104
  93.5 38.9 %all-gather.1 = bf16[32,1,128]{2,1,0:T(2,128)(2,1)S(1)} all-gather(bf16[1,1,128]{2,1,0:T(2,128)(2,1)S(1)} %convert_bitcast_fusion.1), channel_id=1, replica_groups=mesh['dp'=4,'seq'=8] {'dp','seq'}, dimensions={0}, use_global_device_ids=true | all-gather | bytes 8448 | tf_op jit(solution)/shard_map/all_gather | solution.py:150
  136.8 26.8 %all-gather.19.cloned.1.call-done = bf16[4096,1024]{1,0:T(8,128)(2,1)} async-done(((bf16[128,1024]{1,0:T(8,128)(2,1)}), bf16[4096,1024]{1,0:T(8,128)(2,1)}) %all-gather.19.cloned.1.call-update) | async-done | bytes 8388624 | tf_op jit(solution)/shard_map/all_gather | solution.py:149
  163.6 7.7 fusion.118
  171.3 44.7 %all-gather.13.cloned.1.call-done = bf16[2,1024,16,64]{1,0,3,2:T(2,128)(2,1)} async-done(((bf16[2,128,16,64]{1,0,3,2:T(2,128)(2,1)}), bf16[2,1024,16,64]{1,0,3,2:T(2,128)(2,1)}) %all-gather.13.cloned.1.call-update) | async-done | bytes 4194320 | tf_op jit(solution)/shard_map/all_gather | solution.py:127
  216.0 5.5 copy.88
  221.5 48.1 %all-gather.11.cloned.1.call-done = bf16[2,1024,16,64]{1,0,3,2:T(2,128)(2,1)} async-done(((bf16[2,128,16,64]{1,0,3,2:T(2,128)(2,1)}), bf16[2,1024,16,64]{1,0,3,2:T(2,128)(2,1)}) %all-gather.11.cloned.1.call-update) | async-done | bytes 4194320 | tf_op jit(solution)/shard_map/all_gather | solution.py:128
  269.6 5.5 copy.86
  275.2 30.2 %while.24 = (s32[]{:T(128)}, bf16[2,128,16,64]{1,3,2,0:T(8,128)(2,1)S(1)}, bf16[2,1024,16,64]{1,3,2,0:T(8,128)(2,1)}, s32[1024]{0:T(1024)S(1)}, s32[128]{0:T(128...) while((s32[]{:T(128)}, ...), condition=%wide.region_7.8_spmd, body=%wide.region_4.7_spmd.sunk | while | flops 553912320 | bytes 55603856 | solution.py:143
  279.6 5.6 fusion.161
  285.2 5.1 fusion.162
  294.7 5.6 fusion.161
  300.3 5.1 fusion.162
  306.8 22.7 %all-gather.15.cloned.1.call-done = bf16[1024,1024]{1,0:T(8,128)(2,1)} async-done(((bf16[32,1024]{1,0:T(8,128)(2,1)}), bf16[1024,1024]{1,0:T(8,128)(2,1)}) %all-gather.15.cloned.1.call-update) | async-done | bytes 2097168 | tf_op jit(solution)/shard_map/all_gather | solution.py:105
  332.4 76.8 %all-gather.17.cloned.1.call-done = bf16[1024,4096]{1,0:T(8,128)(2,1)} async-done(((bf16[32,4096]{1,0:T(8,128)(2,1)}), bf16[1024,4096]{1,0:T(8,128)(2,1)}) %all-gather.17.cloned.1.call-update) | async-done | bytes 8388624 | tf_op jit(solution)/shard_map/all_gather | solution.py:148
  409.2 12.7 convert_reduce_fusion
  429.7 41.3 %while.25 = (s32[]{:T(128)}, bf16[2,128,16,64]{1,3,2,0:T(8,128)(2,1)S(1)}, f32[2,1024,16,64]{1,3,2,0:T(8,128)}, f32[2,1024,16,64]{1,3,2,0:T(8,128)}, bf16[2,1024...) while((s32[]{:T(128)}, ...), condition=%wide.region_16.17_spmd, body=%wide.region_12.16_spmd.sunk | while | flops 1375076352 | bytes 129826496 | solution.py:220
  476.1 83.2 %reduce-scatter.12.cloned.1.call-done = f32[2,128,16,64]{1,3,2,0:T(8,128)} async-done(((f32[2,1024,16,64]{1,3,2,0:T(8,128)}), f32[2,128,16,64]{1,3,2,0:T(8,128)}) %reduce-scatter.12.cloned.1.call-update) | async-done | bytes 1048592 | tf_op jit(solution)/shard_map/reduce_scatter | solution.py:225
  560.8 88.7 %reduce-scatter.10.cloned.1.call-done = f32[2,128,16,64]{1,3,2,0:T(8,128)} async-done(((f32[2,1024,16,64]{1,3,2,0:T(8,128)}), f32[2,128,16,64]{1,3,2,0:T(8,128)}) %reduce-scatter.10.cloned.1.call-update) | async-done | bytes 1048592 | tf_op jit(solution)/shard_map/reduce_scatter | solution.py:224
  652.3 4.9 fusion.102
  659.9 9.8 fusion.100
  669.8 10.8 fusion.101
  681.0 7.4 fusion.119
  689.8 38.4 %all-reduce = f32[4096]{0:T(1024)S(1)} all-reduce(f32[4096]{0:T(1024)S(1)} %copy-done.45), channel_id=9, replica_groups=mesh['dp'=4,'seq'=8] {'dp','seq'}, use_global_device_ids=true, to_apply=%region_40.41.clone | all-reduce | flops 4096 | bytes 32768
  728.8 8.5 fusion.74
  737.3 55.6 %reduce-scatter.16.cloned.1.call-done = f32[32,1024]{1,0:T(8,128)} async-done(((f32[1024,1024]{1,0:T(8,128)}), f32[32,1024]{1,0:T(8,128)}) %reduce-scatter.16.cloned.1.call-update) | async-done | bytes 131088 | tf_op jit(solution)/shard_map/reduce_scatter | solution.py:255
  795.0 131.5 %reduce-scatter.22.cloned.1.call-done = f32[32,8]{1,0:T(8,128)} async-done(((f32[1024,8]{1,0:T(8,128)}), f32[32,8]{1,0:T(8,128)}) %reduce-scatter.22.cloned.1.call-update) | async-done | bytes 1040
  928.0 184.0 %reduce-scatter.18.cloned.1.call-done = f32[32,4096]{1,0:T(8,128)} async-done(((f32[1024,4096]{1,0:T(8,128)}), f32[32,4096]{1,0:T(8,128)}) %reduce-scatter.18.cloned.1.call-update) | async-done | bytes 524304 | tf_op jit(solution)/shard_map/reduce_scatter | solution.py:180
  1113.8 184.8 %reduce-scatter.20.cloned.1.call-done = f32[128,1024]{1,0:T(8,128)} async-done(((f32[4096,1024]{1,0:T(8,128)}), f32[128,1024]{1,0:T(8,128)}) %reduce-scatter.20.cloned.1.call-update) | async-done | bytes 524304 | tf_op jit(solution)/shard_map/reduce_scatter | solution.py:181
  1300.4 158.4 %reduce-scatter.14.cloned.1.call-done = f32[32,3072]{1,0:T(8,128)} async-done(((f32[1024,3072]{1,0:T(8,128)}), f32[32,3072]{1,0:T(8,128)}) %reduce-scatter.14.cloned.1.call-update) | async-done | bytes 393232 | tf_op jit(solution)/shard_map/reduce_scatter | solution.py:254
  1467.6 39.8 %psum.7 = f32[]{:T(128)} all-reduce(f32[]{:T(128)S(6)} %add.310), channel_id=1, replica_groups=mesh['dp'=4,'seq'=8] {'dp','seq'}, use_global_device_ids=true, to_apply=%region_42.43 | all-reduce | flops 1 | bytes 8 | tf_op jit(solution)/shard_map/psum | solution.py:270
  (265 shorter events, 124.4 us)
Async XLA Ops:
  7.2 76.7 %all-gather.9.cloned.1.call-start = ((), (), s32[]{:S(2)}) async-start(), calls=%async_computation.7 | async-start | bytes 6488064 | tf_op jit(solution)/shard_map/all_gather | solution.py:104
  9.0 154.7 %all-gather.19.cloned.1.call-start = ((), (), s32[]{:S(2)}) async-start(), calls=%async_computation.12 | async-start | bytes 8650752 | tf_op jit(solution)/shard_map/all_gather | solution.py:149
  10.8 205.2 %all-gather.13.cloned.1.call-start = ((), (), s32[]{:S(2)}) async-start(), calls=%async_computation.9 | async-start | bytes 4718592 | tf_op jit(solution)/shard_map/all_gather | solution.py:127
  56.1 353.0 %copy-start.32 = (f32[1024,1]{0,1:T(1,128)}, f32[1024,1]{0,1:T(1,128)S(1)}, u32[]{:S(2)}) copy-start(f32[1024,1]{0,1:T(1,128)S(1)} %get-tuple-element.286) | copy-start | bytes 12292
  56.1 368.9 %copy-start.30 = (f32[1024,1]{0,1:T(1,128)}, f32[1024,1]{0,1:T(1,128)S(1)}, u32[]{:S(2)}) copy-start(f32[1024,1]{0,1:T(1,128)S(1)} %get-tuple-element.284) | copy-start | bytes 12292
  90.7 178.9 %all-gather.11.cloned.1.call-start = ((), (), s32[]{:S(2)}) async-start(), calls=%async_computation.8 | async-start | bytes 4718592 | tf_op jit(solution)/shard_map/all_gather | solution.py:128
  91.9 237.6 %all-gather.15.cloned.1.call-start = ((), (), s32[]{:S(2)}) async-start(), calls=%async_computation.10 | async-start | bytes 2162688 | tf_op jit(solution)/shard_map/all_gather | solution.py:105
  92.6 316.6 %all-gather.17.cloned.1.call-start = ((), (), s32[]{:S(2)}) async-start(), calls=%async_computation.11 | async-start | bytes 8650752 | tf_op jit(solution)/shard_map/all_gather | solution.py:148
  93.4 465.9 %reduce-scatter.12.cloned.1.call-start = ((), (), s32[]{:S(2)}) async-start(), calls=%async_computation.14 | async-start | bytes 9437184 | tf_op jit(solution)/shard_map/reduce_scatter | solution.py:225
  133.5 292.0 %copy-start.5 = (f32[2,128,1024]{2,1,0:T(8,128)}, f32[2,128,1024]{2,1,0:T(8,128)S(1)}, u32[]{:S(2)}) copy-start(f32[2,128,1024]{2,1,0:T(8,128)S(1)} %get-tuple-element.283) | copy-start | bytes 3145732
  275.2 54.2 %copy-start.1 = (bf16[2,128,1024]{2,1,0:T(8,128)(2,1)S(1)}, bf16[2,128,1024]{2,1,0:T(8,128)(2,1)}, u32[]{:S(2)}) copy-start(bf16[2,128,1024]{2,1,0:T(8,128)(2,1)} %param.28) | copy-start | bytes 1572868
  332.1 93.0 %copy-start.3 = (f32[256,1024]{1,0:T(8,128)}, f32[256,1024]{1,0:T(8,128)S(1)}, u32[]{:S(2)}) copy-start(f32[256,1024]{1,0:T(8,128)S(1)} %get-tuple-element.301) | copy-start | bytes 3145732
  332.1 93.0 %copy-start.36 = (f32[256]{0:T(256)}, f32[256]{0:T(256)S(1)}, u32[]{:S(2)}) copy-start(f32[256]{0:T(256)S(1)} %broadcast_multiply_fusion) | copy-start | bytes 3076
  332.4 92.7 %copy-start.38 = (f32[256]{0:T(256)}, f32[256]{0:T(256)S(1)}, u32[]{:S(2)}) copy-start(f32[256]{0:T(256)S(1)} %fusion.95) | copy-start | bytes 3076
  470.9 178.6 %reduce-scatter.10.cloned.1.call-start = ((), (), s32[]{:S(2)}) async-start(), calls=%async_computation.13 | async-start | bytes 9437184 | tf_op jit(solution)/shard_map/reduce_scatter | solution.py:224
  471.7 321.2 %reduce-scatter.16.cloned.1.call-start = ((), (), s32[]{:S(2)}) async-start(), calls=%async_computation.16 | async-start | bytes 4325376 | tf_op jit(solution)/shard_map/reduce_scatter | solution.py:255
  474.9 451.7 %reduce-scatter.22.cloned.1.call-start = ((), (), s32[]{:S(2)}) async-start(), calls=%async_computation.19 | async-start | bytes 540672
  476.0 176.2 %copy-start.2 = (bf16[2,128,1024]{2,1,0:T(8,128)(2,1)S(1)}, bf16[2,128,1024]{2,1,0:T(8,128)(2,1)}, u32[]{:S(2)}) copy-start(bf16[2,128,1024]{2,1,0:T(8,128)(2,1)} %param.28) | copy-start | bytes 1572868
  476.0 176.2 %copy-start.35 = (f32[1024,1]{0,1:T(1,128)S(1)}, f32[1024,1]{0,1:T(1,128)}, u32[]{:S(2)}) copy-start(f32[1024,1]{0,1:T(1,128)} %copy-done.34) | copy-start | bytes 12292
  476.0 176.2 %copy-start.47 = (f32[256]{0:T(256)S(1)}, f32[256]{0:T(256)}, u32[]{:S(2)}) copy-start(f32[256]{0:T(256)} %copy-done.46) | copy-start | bytes 3076
  659.8 452.1 %reduce-scatter.18.cloned.1.call-start = ((), (), s32[]{:S(2)}) async-start(), calls=%async_computation.17 | async-start | bytes 17301504 | tf_op jit(solution)/shard_map/reduce_scatter | solution.py:180
  669.8 628.8 %reduce-scatter.20.cloned.1.call-start = ((), (), s32[]{:S(2)}) async-start(), calls=%async_computation.18 | async-start | bytes 17301504 | tf_op jit(solution)/shard_map/reduce_scatter | solution.py:181
  680.7 778.1 %reduce-scatter.14.cloned.1.call-start = ((), (), s32[]{:S(2)}) async-start(), calls=%async_computation.15 | async-start | bytes 12976128 | tf_op jit(solution)/shard_map/reduce_scatter | solution.py:254
  728.8 735.6 %copy-start.6 = (f32[2,128,1024]{2,1,0:T(8,128)S(1)}, f32[2,128,1024]{2,1,0:T(8,128)}, u32[]{:S(2)}) copy-start(f32[2,128,1024]{2,1,0:T(8,128)} %copy-done.5) | copy-start | bytes 3145732
  737.3 772.8 %copy-start.44 = (f32[32,8]{0,1:T(8,128)S(1)}, f32[32,8]{0,1:T(8,128)}, u32[]{:S(2)}) copy-start(f32[32,8]{0,1:T(8,128)} %param.38) | copy-start | bytes 3076
  737.3 774.8 %copy-start.28 = (f32[32,1024]{1,0:T(8,128)S(1)}, f32[32,1024]{1,0:T(8,128)}, u32[]{:S(2)}) copy-start(f32[32,1024]{1,0:T(8,128)} %param.35) | copy-start | bytes 393220
  737.3 777.3 %copy-start.23 = (f32[32,3072]{1,0:T(8,128)S(1)}, f32[32,3072]{1,0:T(8,128)}, u32[]{:S(2)}) copy-start(f32[32,3072]{1,0:T(8,128)} %param.34) | copy-start | bytes 1179652
  1458.8 55.8 %copy-start.24 = (f32[32,3072]{1,0:T(8,128)S(1)}, f32[32,3072]{1,0:T(8,128)}, u32[]{:S(2)}) copy-start(f32[32,3072]{1,0:T(8,128)} %reduce-scatter.14.cloned.1.call-done) | copy-start | bytes 1179652
  1464.4 53.1 %copy-start.17 = (f32[32,4096]{1,0:T(8,128)S(1)}, f32[32,4096]{1,0:T(8,128)}, u32[]{:S(2)}) copy-start(f32[32,4096]{1,0:T(8,128)} %param.36) | copy-start | bytes 1572868
  1467.6 53.2 %copy-start.18 = (f32[128,1024]{1,0:T(8,128)S(1)}, f32[128,1024]{1,0:T(8,128)}, u32[]{:S(2)}) copy-start(f32[128,1024]{1,0:T(8,128)} %param.37) | copy-start | bytes 1572868
  1467.6 53.2 %copy-start.21 = (f32[128,1024]{1,0:T(8,128)S(1)}, f32[128,1024]{1,0:T(8,128)}, u32[]{:S(2)}) copy-start(f32[128,1024]{1,0:T(8,128)} %reduce-scatter.20.cloned.1.call-done) | copy-start | bytes 1572868
  1467.6 53.2 %copy-start.25 = (f32[128,1024]{1,0:T(8,128)S(1)}, f32[128,1024]{1,0:T(8,128)}, u32[]{:S(2)}) copy-start(f32[128,1024]{1,0:T(8,128)} %param.49) | copy-start | bytes 1572868
  (45 other events, 576.2 us)
Sparse Core Ops, SparseCore 0:
  11.6 72.2 all-gather.8
  87.5 76.1 all-gather.18
  165.8 50.1 all-gather.12
  218.0 51.5 all-gather.10
  273.0 56.4 all-gather.14
  332.9 76.2 all-gather.16
  471.1 88.1 reduce-scatter.11
  561.6 87.9 reduce-scatter.9
  651.9 141.0 reduce-scatter.15
  795.6 130.9 reduce-scatter.21
  929.0 182.9 reduce-scatter.17
  1114.2 184.3 reduce-scatter.19
  1305.7 153.0 reduce-scatter.13
where the time goes:
time: 1540 us; the launch traced here: 1530 us
  waiting for transfers between devices  1130 us (73%)
  blocking collectives  161 us (10%)
  matrix products  116 us (8%)
  other arithmetic  66.8 us (4%)
  local copies, waits for them, and re-layouts  34.2 us (2%)
  between operations  21.5 us (1%)
    reduce_scatter x1, waiting for transfers between devices, per_device(): lax.psum_scatter(grad_shrink, ('dp', 'seq'), scatter_dimension=0, tiled=T...  185 us
    reduce_scatter x1, waiting for transfers between devices, per_device(): lax.psum_scatter(grad_expand, ('dp', 'seq'), scatter_dimension=0, tiled=T...  184 us
    reduce_scatter x1, waiting for transfers between devices, per_device(): lax.psum_scatter(grad_qkv_w, ('dp', 'seq'), scatter_dimension=0, tiled=True)  158 us
    unnamed x14, waiting for transfers between devices  132 us
    reduce_scatter x1, waiting for transfers between devices, per_device(): lax.psum_scatter(key_terms, 'seq', scatter_dimension=1, tiled=True)  88.7 us
    reduce_scatter x1, waiting for transfers between devices, per_device(): lax.psum_scatter(value_terms, 'seq', scatter_dimension=1, tiled=True)  83.2 us
    all_gather x1, waiting for transfers between devices, per_device(): lax.all_gather(w_expand.astype(low_type), ('dp', 'seq'), axis=0, tiled=True)  76.8 us
    reduce_scatter x1, waiting for transfers between devices, per_device(): lax.psum_scatter(grad_proj, ('dp', 'seq'), scatter_dimension=0, tiled=True)  55.6 us
  transfers between devices with their start and end apart: 13, of which 13 were waited for; matrix products, arithmetic and copies ran while one was open for 9% of the time, Pallas kernels for 0%

commit v1 on v0

--- a/solution.py
+++ b/solution.py
@@ -1,12 +1,16 @@
+import functools
 import math
 
 import jax
 import jax.numpy as jnp
 from jax import lax
+from jax.experimental import pallas as pl
+from jax.experimental.pallas import tpu as pltpu
 from jax.sharding import PartitionSpec as P
 
 HEADS = 16
 HD = 64
+MESH = pl.DeviceIdType.MESH
 
 
 norm_eps = 1e-05
@@ -18,6 +22,378 @@
 clip_bound = 1.0
 
 
+def flip(index, mask):
+    return index + mask * (1 - 2 * ((index // mask) % 2))
+
+
+class Place:
+    def __init__(self, dp_size, seq_size):
+        self.dp_size = dp_size
+        self.depth = seq_size // 2
+        self.bits = dp_size.bit_length() - 1
+        self.dp = lax.axis_index("dp")
+        seq = lax.axis_index("seq")
+        self.z = seq // 2
+        self.core = seq % 2
+        self.masks = self.masks_of(self.core)
+
+    def masks_of(self, core):
+        return [
+            (1 - core) * 2 ** (k % self.bits) + core * 2 ** ((k + 1) % self.bits)
+            for k in range(self.bits)
+        ]
+
+    def leaving(self, core_masks=None):
+        masks = self.masks if core_masks is None else core_masks
+        order = []
+        for k in range(self.bits - 1, -1, -1):
+            order = order + self.span(flip(self.dp, masks[k]), k, masks)
+        return order + [self.dp]
+
+    def cube(self, k):
+        return (flip(self.dp, self.masks[k]), self.z * 2 + self.core)
+
+    def span(self, start, k, masks=None):
+        found = [start]
+        for mask in (self.masks if masks is None else masks)[:k]:
+            found = found + [flip(one, mask) for one in found]
+        return found
+
+    def sibling(self):
+        return (self.dp, self.z * 2 + 1 - self.core)
+
+    def line(self, j):
+        return (self.dp, ((self.z + j) % self.depth) * 2 + self.core)
+
+
+def greet(peers):
+    barrier = pltpu.get_barrier_semaphore()
+    for peer in peers:
+        pl.semaphore_signal(barrier, inc=1, device_id=peer, device_id_type=MESH)
+    pl.semaphore_wait(barrier, len(peers))
+
+
+def gather_kernel(dp_size, seq_size, count, *refs):
+    sources, fulls = refs[:count], refs[count : 2 * count]
+    local_sem, line_send, cube_send, pair_send, arrive = refs[2 * count :]
+    at = Place(dp_size, seq_size)
+    depth, bits, dp, z, core = at.depth, at.bits, at.dp, at.z, at.core
+    greet(
+        [at.line(j) for j in range(1, depth)] + [at.cube(k) for k in range(bits)] + [at.sibling()]
+    )
+    pending = []
+
+    def send(a, source, row, level, peer, sem):
+        copy = pltpu.make_async_remote_copy(
+            src_ref=source,
+            dst_ref=fulls[a].at[row, level, core],
+            send_sem=sem,
+            recv_sem=arrive.at[a, row, level, core],
+            device_id=peer,
+            device_id_type=MESH,
+        )
+        copy.start()
+        pending.append(copy)
+
+    def received(a, row, level, side):
+        block = fulls[a].at[row, level, side]
+        pltpu.make_async_copy(block, block, arrive.at[a, row, level, side]).wait()
+
+    def pass_on(a, source, row, slot, level, first):
+        for k in range(first, bits):
+            send(a, source, row, level, at.cube(k), cube_send.at[a, k, slot, level])
+        send(a, source, row, level, at.sibling(), pair_send.at[a, slot, level])
+
+    for a in range(count):
+        for j in range(1, depth):
+            send(a, sources[a], dp, z, at.line(j), line_send.at[a, j - 1])
+        pass_on(a, sources[a], dp, 0, z, 0)
+    locals_ = []
+    for a in range(count):
+        copy = pltpu.make_async_copy(sources[a], fulls[a].at[dp, z, core], local_sem.at[a])
+        copy.start()
+        locals_.append(copy)
+
+    def line_stage(a):
+        for j in range(depth - 1, 0, -1):
+            level = (z + j) % depth
+            received(a, dp, level, core)
+            pass_on(a, fulls[a].at[dp, level, core], dp, 0, level, 0)
+
+    def cube_stage(a, k):
+        for slot, row in enumerate(at.span(flip(dp, at.masks[k]), k)):
+            for j in range(depth):
+                level = (z + j) % depth
+                received(a, row, level, core)
+                pass_on(a, fulls[a].at[row, level, core], row, 2**k + slot, level, k + 1)
+
+    stages = bits + 1
+    for step in range(count + stages - 1):
+        for stage in range(stages):
+            a = step - stage
+            if 0 <= a < count:
+                if stage == 0:
+                    line_stage(a)
+                else:
+                    cube_stage(a, stage - 1)
+    for a in range(count):
+        for row in range(dp_size):
+            for level in range(depth):
+                received(a, row, level, 1 - core)
+    for copy in locals_:
+        copy.wait()
+    for copy in pending:
+        copy.wait_send()
+
+
+def gather_all(blocks, dp_size, seq_size):
+    count = len(blocks)
+    depth, bits = seq_size // 2, dp_size.bit_length() - 1
+    shapes = [
+        jax.ShapeDtypeStruct((dp_size, depth, 2) + block.shape, block.dtype) for block in blocks
+    ]
+    return pl.pallas_call(
+        functools.partial(gather_kernel, dp_size, seq_size, count),
+        out_shape=shapes,
+        in_specs=[pl.BlockSpec(memory_space=pl.ANY)] * count,
+        out_specs=[pl.BlockSpec(memory_space=pl.ANY)] * count,
+        scratch_shapes=[
+            pltpu.SemaphoreType.DMA((count,)),
+            pltpu.SemaphoreType.DMA((count, depth - 1)),
+            pltpu.SemaphoreType.DMA((count, bits, dp_size, depth)),
+            pltpu.SemaphoreType.DMA((count, dp_size, depth)),
+            pltpu.SemaphoreType.DMA((count, dp_size, depth, 2)),
+        ],
+        compiler_params=pltpu.CompilerParams(collective_id=0, has_side_effects=True),
+        name="gather_all",
+    )(*blocks)
+
+
+def scatter_kernel(dp_size, seq_size, count, *refs):
+    at = Place(dp_size, seq_size)
+    depth, bits, dp, z, core = at.depth, at.bits, at.dp, at.z, at.core
+    grads, outs, norm_out = refs[:count], refs[count : 2 * count], refs[2 * count]
+    scratch = refs[2 * count + 1 :]
+    own, pair = scratch[:count], scratch[count : 2 * count]
+    cube = [scratch[(2 + k) * count : (3 + k) * count] for k in range(bits)]
+    line = scratch[(2 + bits) * count : (3 + bits) * count]
+    seq_part, dp_part, mine = scratch[(3 + bits) * count : (3 + bits) * count + 3]
+    (own_sem, pair_send, pair_recv, cube_send, cube_recv, line_send, line_recv) = scratch[
+        (3 + bits) * count + 3 : (3 + bits) * count + 10
+    ]
+    norm_send, norm_recv = scratch[(3 + bits) * count + 10 :]
+    seq = z * 2 + core
+    seq_peers = [(dp, (seq + j) % seq_size) for j in range(1, seq_size)]
+    dp_peers = [((dp + j) % dp_size, seq) for j in range(1, dp_size)]
+    greet(seq_peers + dp_peers)
+    pending = []
+
+    order = at.leaving()
+    theirs = at.leaving(at.masks_of(1 - core))
+    for a in range(count):
+        for spot, row in enumerate(order):
+            copy = pltpu.make_async_remote_copy(
+                src_ref=grads[a].at[theirs[spot], :, 1 - core],
+                dst_ref=pair[a].at[theirs[spot]],
+                send_sem=pair_send.at[a, spot],
+                recv_sem=pair_recv.at[a, theirs[spot]],
+                device_id=at.sibling(),
+                device_id_type=MESH,
+            )
+            copy.start()
+            pending.append(copy)
+            pltpu.make_async_copy(
+                grads[a].at[row, :, core], own[a].at[row], own_sem.at[a, spot]
+            ).start()
+
+    def ready(a, spot):
+        row = order[spot]
+        pltpu.make_async_copy(grads[a].at[row, :, core], own[a].at[row], own_sem.at[a, spot]).wait()
+        pltpu.make_async_copy(pair[a].at[row], pair[a].at[row], pair_recv.at[a, row]).wait()
+
+    def total(a, row, level, rows, hops):
+        value = own[a][row, level, rows].astype(jnp.float32)
+        value = value + pair[a][row, level, rows].astype(jnp.float32)
+        for k, slot in hops:
+            value = value + cube[k][a][slot, level, rows].astype(jnp.float32)
+        return value
+
+    def each_chunk(a, body):
+        height = own[a].shape[2]
+        step = min(16, height)
+        if step == height:
+            body(pl.ds(0, step))
+        else:
+
+            def one(i, carry):
+                body(pl.ds(pl.multiple_of(i * step, step), step))
+                return carry
+
+            lax.fori_loop(0, height // step, one, 0)
+
+    def fold(a, row, hops):
+        for level in range(depth):
+
+            def body(rows, level=level):
+                own[a][row, level, rows] = total(a, row, level, rows, hops).astype(own[a].dtype)
+
+            each_chunk(a, body)
+
+    def cube_stage(a, k):
+        leave = at.span(flip(dp, at.masks[k]), k)
+        for slot, row in enumerate(leave):
+            spot = spot_of(bits, k, slot)
+            ready(a, spot)
+            landed = [(q, landing_slot(bits, k, slot, q)) for q in range(k + 1, bits)]
+            for q, hop_slot in landed:
+                block = cube[q][a].at[hop_slot]
+                pltpu.make_async_copy(block, block, cube_recv.at[a, q, hop_slot]).wait()
+            fold(a, row, landed)
+            copy = pltpu.make_async_remote_copy(
+                src_ref=own[a].at[row],
+                dst_ref=cube[k][a].at[slot],
+                send_sem=cube_send.at[a, k, slot],
+                recv_sem=cube_recv.at[a, k, slot],
+                device_id=at.cube(k),
+                device_id_type=MESH,
+            )
+            copy.start()
+            pending.append(copy)
+
+    all_hops = [(q, 0) for q in range(bits)]
+
+    def line_stage(a):
+        ready(a, len(order) - 1)
+        for q, hop_slot in all_hops:
+            block = cube[q][a].at[hop_slot]
+            pltpu.make_async_copy(block, block, cube_recv.at[a, q, hop_slot]).wait()
+        for j in range(1, depth):
+            level = (z + j) % depth
+
+            def body(rows, level=level):
+                own[a][dp, level, rows] = total(a, dp, level, rows, all_hops).astype(own[a].dtype)
+
+            each_chunk(a, body)
+            copy = pltpu.make_async_remote_copy(
+                src_ref=own[a].at[dp, level],
+                dst_ref=line[a].at[j - 1],
+                send_sem=line_send.at[a, j - 1],
+                recv_sem=line_recv.at[a, j - 1],
+                device_id=at.line(j),
+                device_id_type=MESH,
+            )
+            copy.start()
+            pending.append(copy)
+
+    mine[...] = jnp.zeros_like(mine)
+
+    def final_stage(a):
+        for j in range(1, depth):
+            block = line[a].at[j - 1]
+            pltpu.make_async_copy(block, block, line_recv.at[a, j - 1]).wait()
+
+        def body(rows):
+            value = total(a, dp, z, rows, all_hops)
+            for j in range(1, depth):
+                value = value + line[a][j - 1, rows].astype(jnp.float32)
+            outs[a][rows] = value
+            squares = value * value
+            height, width = squares.shape
+            folded = squares.reshape(height // 8, 8, width).sum(0)
+            part = folded[:, :128]
+            for lane in range(1, width // 128):
+                part = part + folded[:, lane * 128 : (lane + 1) * 128]
+            mine[...] += part
+
+        each_chunk(a, body)
+
+    stages = bits + 2
+    for step in range(count + stages - 1):
+        for stage in range(stages):
+            a = step - stage
+            if 0 <= a < count:
+                if stage < bits:
+                    cube_stage(a, bits - 1 - stage)
+                elif stage == bits:
+                    line_stage(a)
+                else:
+                    final_stage(a)
+
+    def exchange(peers, parts, base):
+        copies = []
+        for i, peer in enumerate(peers):
+            copy = pltpu.make_async_remote_copy(
+                src_ref=mine,
+                dst_ref=parts.at[i],
+                send_sem=norm_send.at[base + i],
+                recv_sem=norm_recv.at[base + i],
+                device_id=peer,
+                device_id_type=MESH,
+            )
+            copy.start()
+            copies.append(copy)
+        for copy in copies:
+            copy.wait()
+
+    exchange(seq_peers, seq_part, 0)
+    value = mine[...]
+    for i in range(seq_size - 1):
+        value = value + seq_part[i]
+    mine[...] = value
+    exchange(dp_peers, dp_part, seq_size - 1)
+    value = mine[...]
+    for i in range(dp_size - 1):
+        value = value + dp_part[i]
+    norm_out[...] = value
+    for copy in pending:
+        copy.wait_send()
+
+
+def spot_of(bits, k, slot):
+    return sum(2**q for q in range(k + 1, bits)) + slot
+
+
+def landing_slot(bits, k, slot, q):
+    return 2**k + slot
+
+
+def scatter_all(grads, dp_size, seq_size):
+    count = len(grads)
+    depth, bits = seq_size // 2, dp_size.bit_length() - 1
+    tails = [grad.shape[3:] for grad in grads]
+    kinds = [grad.dtype for grad in grads]
+    scratch = []
+    for lead in [(dp_size, depth)] * 2 + [(2**k, depth) for k in range(bits)] + [(depth - 1,)]:
+        scratch += [pltpu.VMEM(lead + tail, kind) for tail, kind in zip(tails, kinds)]
+    scratch += [
+        pltpu.VMEM((seq_size - 1, 8, 128), jnp.float32),
+        pltpu.VMEM((dp_size - 1, 8, 128), jnp.float32),
+        pltpu.VMEM((8, 128), jnp.float32),
+        pltpu.SemaphoreType.DMA((count, dp_size)),
+        pltpu.SemaphoreType.DMA((count, dp_size)),
+        pltpu.SemaphoreType.DMA((count, dp_size)),
+        pltpu.SemaphoreType.DMA((count, bits, dp_size // 2)),
+        pltpu.SemaphoreType.DMA((count, bits, dp_size // 2)),
+        pltpu.SemaphoreType.DMA((count, depth - 1)),
+        pltpu.SemaphoreType.DMA((count, depth - 1)),
+        pltpu.SemaphoreType.DMA((seq_size + dp_size - 2,)),
+        pltpu.SemaphoreType.DMA((seq_size + dp_size - 2,)),
+    ]
+    shapes = [jax.ShapeDtypeStruct(tail, jnp.float32) for tail in tails]
+    shapes.append(jax.ShapeDtypeStruct((8, 128), jnp.float32))
+    return pl.pallas_call(
+        functools.partial(scatter_kernel, dp_size, seq_size, count),
+        out_shape=shapes,
+        in_specs=[pl.BlockSpec(memory_space=pl.ANY)] * count,
+        out_specs=[pl.BlockSpec(memory_space=pltpu.VMEM)] * (count + 1),
+        scratch_shapes=scratch,
+        compiler_params=pltpu.CompilerParams(
+            collective_id=1, has_side_effects=True, vmem_limit_bytes=56 << 20
+        ),
+        name="scatter_all",
+    )(*grads)
+
+
 def layer_norm(values, gain_vec, shift_vec):
     centered = values - jnp.mean(values, axis=-1, keepdims=True)
     variance = jnp.mean(centered * centered, axis=-1, keepdims=True)
@@ -58,6 +434,23 @@
     exp_scores = jnp.exp(scores - row_max)
     row_total = jnp.sum(exp_scores, axis=-1, keepdims=True)
     return (exp_scores / row_total, row_max + jnp.log(row_total))
+
+
+def pack_small(vec_cols, bias, devices):
+    wide = vec_cols.shape[1] // devices
+    parts = vec_cols.reshape(8, devices, wide).transpose(1, 0, 2).reshape(devices, 8 * wide)
+    flat = jnp.concatenate([parts, bias.reshape(devices, -1)], axis=1)
+    length = flat.shape[1]
+    padded = -(-length // 2048) * 2048
+    flat = jnp.pad(flat, ((0, 0), (0, padded - length)))
+    return flat.reshape(devices, padded // 128, 128)
+
+
+def unpack_small(packed, devices, model_width, hidden):
+    flat = packed.reshape(devices, -1)
+    wide, high = model_width // devices, hidden // devices
+    cols = flat[:, : 8 * wide].reshape(devices, 8, wide).transpose(1, 0, 2)
+    return cols.reshape(8, model_width), flat[:, 8 * wide : 8 * wide + high].reshape(hidden)
 
 
 def per_device(
@@ -88,8 +481,12 @@
 ):
     low_type = jnp.bfloat16
     wide_type = jnp.float32
+    dp_size, seq_size = lax.axis_size("dp"), lax.axis_size("seq")
+    devices = dp_size * seq_size
+    lead = (dp_size, seq_size // 2, 2)
     seqs_here, local_slots, model_width = inputs.shape
-    total_slots = local_slots * lax.axis_size("seq")
+    hidden = w_expand.shape[1]
+    total_slots = local_slots * seq_size
     block_len = total_slots // block_order.shape[0]
     score_scale = 1.0 / math.sqrt(HD)
     token_count = seqs_here * local_slots
@@ -100,20 +497,37 @@
     key_pos = slot_positions(jnp.arange(total_slots, dtype=jnp.int32), block_order, block_len)
     valid_rows = (local_pos[None, :] < lengths[:, None]).astype(wide_type)
     rows_in = inputs.reshape(token_count, model_width).astype(wide_type)
-    qkv_full, proj_full, vec_full = (
-        lax.all_gather(w_qkv.astype(low_type), ("dp", "seq"), axis=0, tiled=True),
-        lax.all_gather(w_proj.astype(low_type), ("dp", "seq"), axis=0, tiled=True),
-        lax.all_gather(vectors.astype(low_type), ("dp", "seq"), axis=0, tiled=True),
-    )
-    vec_wide = vec_full.astype(wide_type)
-    gain_one = vec_wide[:, 0]
-    shift_one = vec_wide[:, 1]
-    bias_query = vec_wide[:, 2]
-    bias_value = vec_wide[:, 3]
-    bias_proj = vec_wide[:, 4]
-    gain_two = vec_wide[:, 5]
-    shift_two = vec_wide[:, 6]
-    bias_shrink = vec_wide[:, 7]
+
+    small_block = pack_small(vectors.T, bias_expand, 1)[0].astype(low_type)
+    gathered = gather_all(
+        [
+            small_block,
+            w_qkv.astype(low_type),
+            w_proj.astype(low_type),
+            w_expand.astype(low_type),
+            w_shrink.astype(low_type),
+        ],
+        dp_size,
+        seq_size,
+    )
+    qkv_full = gathered[1].reshape(model_width, -1)
+    proj_full = gathered[2].reshape(model_width, -1)
+    expand_full = gathered[3].reshape(model_width, -1)
+    shrink_full = gathered[4].reshape(hidden, -1)
+    vec_cols, bias_full = unpack_small(
+        gathered[0].astype(wide_type), devices, model_width, hidden
+    )
+    (
+        gain_one,
+        shift_one,
+        bias_query,
+        bias_value,
+        bias_proj,
+        gain_two,
+        shift_two,
+        bias_shrink,
+    ) = [vec_cols[i] for i in range(8)]
+
     normed_one = layer_norm(rows_in, gain_one, shift_one).astype(low_type)
     bias_cat = jnp.concatenate([bias_query, jnp.zeros_like(bias_query), bias_value])
     qkv_rows = (jnp.dot(normed_one, qkv_full, preferred_element_type=wide_type) + bias_cat).astype(
@@ -144,15 +558,8 @@
     context_low = context.reshape(token_count, model_width).astype(low_type)
     attn_rows = jnp.dot(context_low, proj_full, preferred_element_type=wide_type) + bias_proj
     resid = rows_in + attn_rows
-    expand_full, shrink_full, bias_full = (
-        lax.all_gather(w_expand.astype(low_type), ("dp", "seq"), axis=0, tiled=True),
-        lax.all_gather(w_shrink.astype(low_type), ("dp", "seq"), axis=0, tiled=True),
-        lax.all_gather(bias_expand.astype(low_type), ("dp", "seq"), axis=0, tiled=True),
-    )
     normed_two = layer_norm(resid, gain_two, shift_two).astype(low_type)
-    pre_act = jnp.dot(normed_two, expand_full, preferred_element_type=wide_type) + bias_full.astype(
-        wide_type
-    )
+    pre_act = jnp.dot(normed_two, expand_full, preferred_element_type=wide_type) + bias_full
     gelu_out, gelu_back = jax.vjp(lambda arg_in: jax.nn.gelu(arg_in, approximate=True), pre_act)
     act_low = gelu_out.astype(low_type)
     layer_rows = (
@@ -164,35 +571,18 @@
     grad_low = grad_rows.astype(low_type)
     grad_shrink = contract_rows(act_low, grad_low)
     grad_bias_shrink = jnp.sum(grad_rows, axis=0)
-    expand_back, shrink_back = (
-        lax.all_gather(w_expand.astype(low_type), ("dp", "seq"), axis=0, tiled=True),
-        lax.all_gather(w_shrink.astype(low_type), ("dp", "seq"), axis=0, tiled=True),
-    )
-    grad_act = contract_cols(grad_low, shrink_back)
+    grad_act = contract_cols(grad_low, shrink_full)
     grad_pre = gelu_back(grad_act)[0].astype(low_type)
     grad_expand = contract_rows(normed_two, grad_pre)
     grad_bias_expand = jnp.sum(grad_pre, axis=0, dtype=wide_type)
-    grad_normed_two = contract_cols(grad_pre, expand_back)
+    grad_normed_two = contract_cols(grad_pre, expand_full)
     norm_two_out, norm_back_two = jax.vjp(layer_norm, resid, gain_two, shift_two)
     grad_resid_part, grad_gain_two, grad_shift_two = norm_back_two(grad_normed_two)
     grad_resid = grad_rows + grad_resid_part
-    grad_expand_mine, grad_shrink_mine, grad_bias_mine = (
-        lax.psum_scatter(grad_expand, ("dp", "seq"), scatter_dimension=0, tiled=True),
-        lax.psum_scatter(grad_shrink, ("dp", "seq"), scatter_dimension=0, tiled=True),
-        lax.psum_scatter(grad_bias_expand, ("dp", "seq"), scatter_dimension=0, tiled=True),
-    )
     grad_attn_low = grad_resid.astype(low_type)
     grad_proj = contract_rows(context_low, grad_attn_low)
     grad_bias_proj = jnp.sum(grad_attn_low, axis=0, dtype=wide_type)
-    qkv_back, proj_back = (
-        lax.all_gather(w_qkv.astype(low_type), ("dp", "seq"), axis=0, tiled=True),
-        lax.all_gather(w_proj.astype(low_type), ("dp", "seq"), axis=0, tiled=True),
-    )
-    grad_context = contract_cols(grad_attn_low, proj_back).astype(low_type).reshape(head_shape)
-    keys_back, values_back = (
-        lax.all_gather(key_local, "seq", axis=1, tiled=True),
-        lax.all_gather(value_local, "seq", axis=1, tiled=True),
-    )
+    grad_context = contract_cols(grad_attn_low, proj_full).astype(low_type).reshape(head_shape)
 
     def backward_one(packed):
         queries, key_block, value_block, grad_ctx, length = packed
@@ -218,7 +608,7 @@
         return (grad_query, key_terms, value_terms)
 
     grad_query, key_terms, value_terms = lax.map(
-        backward_one, (query_all, keys_back, values_back, grad_context, lengths)
+        backward_one, (query_all, keys_all, values_all, grad_context, lengths)
     )
     key_sums, value_sums = (
         lax.psum_scatter(key_terms, "seq", scatter_dimension=1, tiled=True),
@@ -233,11 +623,11 @@
     grad_qkv_w = contract_rows(normed_one, grad_qkv_rows)
     grad_bias_query = jnp.sum(grad_q_low, axis=0, dtype=wide_type)
     grad_bias_value = jnp.sum(grad_v_low, axis=0, dtype=wide_type)
-    grad_normed_one = contract_cols(grad_qkv_rows, qkv_back)
+    grad_normed_one = contract_cols(grad_qkv_rows, qkv_full)
     norm_one_out, norm_back_one = jax.vjp(layer_norm, rows_in, gain_one, shift_one)
     grad_in_part, grad_gain_one, grad_shift_one = norm_back_one(grad_normed_one)
     grad_in_rows = grad_resid + grad_in_part
-    grad_vec = jnp.stack(
+    grad_cols = jnp.stack(
         [
             grad_gain_one,
             grad_shift_one,
@@ -248,13 +638,27 @@
             grad_shift_two,
             grad_bias_shrink,
         ],
-        axis=1,
-    )
-    grad_qkv_mine, grad_proj_mine, grad_vec_mine = (
-        lax.psum_scatter(grad_qkv_w, ("dp", "seq"), scatter_dimension=0, tiled=True),
-        lax.psum_scatter(grad_proj, ("dp", "seq"), scatter_dimension=0, tiled=True),
-        lax.psum_scatter(grad_vec, ("dp", "seq"), scatter_dimension=0, tiled=True),
-    )
+        axis=0,
+    )
+    small_grad = pack_small(grad_cols, grad_bias_expand, devices)
+    scattered = scatter_all(
+        [
+            grad_shrink.astype(low_type).reshape(lead + w_shrink.shape),
+            grad_expand.astype(low_type).reshape(lead + w_expand.shape),
+            grad_proj.astype(low_type).reshape(lead + w_proj.shape),
+            grad_qkv_w.astype(low_type).reshape(lead + w_qkv.shape),
+            small_grad.reshape(lead + small_grad.shape[1:]),
+        ],
+        dp_size,
+        seq_size,
+    )
+    grad_shrink_mine, grad_expand_mine, grad_proj_mine, grad_qkv_mine, small_mine, squares = (
+        scattered
+    )
+    vec_mine, grad_bias_mine = unpack_small(
+        small_mine[None], 1, model_width // devices, hidden // devices
+    )
+    grad_vec_mine = vec_mine.T
     grads = (
         grad_qkv_mine,
         grad_proj_mine,
@@ -266,9 +670,7 @@
     masters = (w_qkv, w_proj, w_expand, w_shrink, vectors, bias_expand)
     firsts = (first_qkv, first_proj, first_expand, first_shrink, first_vectors, first_bias)
     seconds = (second_qkv, second_proj, second_expand, second_shrink, second_vectors, second_bias)
-    square_sum = sum((jnp.sum(gradient * gradient) for gradient in grads))
-    total_square = lax.psum(square_sum, ("dp", "seq"))
-    grad_norm = jnp.sqrt(total_square)
+    grad_norm = jnp.sqrt(jnp.sum(squares))
     clip_factor = clip_bound / jnp.maximum(grad_norm, clip_bound)
     step_float = step_count.astype(wide_type)
     correct_first = 1.0 - beta_first**step_float
@@ -294,57 +696,14 @@
 
 
 def solution(mesh):
+    token_spec = P("dp", "seq", None)
+    matrix_spec = P(("dp", "seq"), None)
+    row_spec = P(("dp", "seq"))
+    group = (matrix_spec,) * 5 + (row_spec,)
     return jax.shard_map(
         per_device,
         mesh=mesh,
-        in_specs=(
-            P("dp", "seq", None),
-            P("dp", "seq", None),
-            P("dp"),
-            P(),
-            P(),
-            P(),
-            P(("dp", "seq"), None),
-            P(("dp", "seq"), None),
-            P(("dp", "seq"), None),
-            P(("dp", "seq"), None),
-            P(("dp", "seq"), None),
-            P(("dp", "seq")),
-            P(("dp", "seq"), None),
-            P(("dp", "seq"), None),
-            P(("dp", "seq"), None),
-            P(("dp", "seq"), None),
-            P(("dp", "seq"), None),
-            P(("dp", "seq")),
-            P(("dp", "seq"), None),
-            P(("dp", "seq"), None),
-            P(("dp", "seq"), None),
-            P(("dp", "seq"), None),
-            P(("dp", "seq"), None),
-            P(("dp", "seq")),
-        ),
-        out_specs=(
-            P("dp", "seq", None),
-            P("dp", "seq", None),
-            P(),
-            P(("dp", "seq"), None),
-            P(("dp", "seq"), None),
-            P(("dp", "seq"), None),
-            P(("dp", "seq"), None),
-            P(("dp", "seq"), None),
-            P(("dp", "seq")),
-            P(("dp", "seq"), None),
-            P(("dp", "seq"), None),
-            P(("dp", "seq"), None),
-            P(("dp", "seq"), None),
-            P(("dp", "seq"), None),
-            P(("dp", "seq")),
-            P(("dp", "seq"), None),
-            P(("dp", "seq"), None),
-            P(("dp", "seq"), None),
-            P(("dp", "seq"), None),
-            P(("dp", "seq"), None),
-            P(("dp", "seq")),
-        ),
+        in_specs=(token_spec, token_spec, P("dp"), P(), P(), P()) + group * 3,
+        out_specs=(token_spec, token_spec, P()) + group * 3,
         check_vma=False,
     )

time: 1540 us -> 730 us (0.47)
  waiting for transfers between devices: 1130 us -> 232 us
  Pallas kernels: 0 us -> 263 us
  blocking collectives: 161 us -> 0 us
  matrix products: 116 us -> 95.6 us
    reduce_scatter x4 -> x0, waiting for transfers between devices: 583 us -> none  [the longest x1 185 us: per_device(): lax.psum_scatter(grad_shrink, ('dp', 'seq'), scatter_dimension=0, tiled=T...]
    pallas_call x0 -> x2, Pallas kernels: none -> 263 us  [the longest x1 145 us: scatter_all(): pl.pallas_call(functools.partial(scatter_kernel, dp_size, seq_size, count...]
    all_gather x4 -> x0, waiting for transfers between devices: 150 us -> none  [the longest x1 76.8 us: per_device(): lax.all_gather(w_expand.astype(low_type), ('dp', 'seq'), axis=0, tiled=True)]
    unnamed x14 -> x4, waiting for transfers between devices: 132 us -> 0.07 us
    all_gather x2 -> x0, blocking collectives: 82.7 us -> none  [the longest x1 43.8 us: per_device(): lax.all_gather(vectors.astype(low_type), ('dp', 'seq'), axis=0, tiled=True)]
    psum x1 -> x0, blocking collectives: 39.8 us -> none  [per_device(): total_square = lax.psum(square_sum, ('dp', 'seq'))]
    unnamed x1 -> x0, blocking collectives: 38.4 us -> none
    reduce_scatter x1, waiting for transfers between devices: 88.7 us -> 52.9 us  [per_device(): lax.psum_scatter(key_terms, 'seq', scatter_dimension=1, tiled=True)]
  transfers between devices with their start and end apart: 13 -> 4, of which waited for: 13 -> 4; matrix products, arithmetic and copies ran while one was open for 9% -> 6% of each run, Pallas kernels for 0% -> 0%
where the time goes in v1:
time: 730 us; the launch traced here: 723 us
  Pallas kernels  263 us (36%)
  waiting for transfers between devices  232 us (32%)
  matrix products  95.6 us (13%)
  other arithmetic  59.2 us (8%)
  local copies, waits for them, and re-layouts  42.7 us (6%)
  between operations  17.5 us (2%)
  starting transfers between devices  12.3 us (2%)
    pallas_call x1, Pallas kernels, scatter_all(): pl.pallas_call(functools.partial(scatter_kernel, dp_size, seq_size, count...  145 us
    pallas_call x1, Pallas kernels, gather_all(): pl.pallas_call(functools.partial(gather_kernel, dp_size, seq_size, count)...  118 us
    reduce_scatter x1, waiting for transfers between devices, per_device(): lax.psum_scatter(value_terms, 'seq', scatter_dimension=1, tiled=True)  87.5 us
    reduce_scatter x1, waiting for transfers between devices, per_device(): lax.psum_scatter(key_terms, 'seq', scatter_dimension=1, tiled=True)  52.9 us
    all_gather x1, waiting for transfers between devices, per_device(): lax.all_gather(key_local, 'seq', axis=1, tiled=True)  48.3 us
    all_gather x1, waiting for transfers between devices, per_device(): lax.all_gather(value_local, 'seq', axis=1, tiled=True)  43.6 us
    sub x4, other arithmetic, softmax_rows(): exp_scores = jnp.exp(scores - row_max)  18.8 us
    dot_general x4, matrix products, contract_rows(): lax.dot_general(left, right, (((0,), (0,)), ((), ())), preferred_element_...  18.6 us
  transfers between devices with their start and end apart: 4, of which 4 were waited for; matrix products, arithmetic and copies ran while one was open for 6% of the time, Pallas kernels for 0%

profile of v1, /device:TPU:0, one launch (start us, length us, event | category | flops | bytes accessed | tf_op | source)
XLA Modules:
  0.0 723.3 jit_solution(4826621540773644363)
XLA Ops:
  16.1 118.0 %gather_all.1 = (bf16[4,4,2,16,128]{4,3,2,1,0:T(8,128)(2,1)}, bf16[4,4,2,32,3072]{4,3,2,1,0:T(8,128)(2,1)}, bf16[4,4,2,32,1024]{4,3,2,1,0:T(8,128)(2,1)}, bf16[4...) custom-call(bf16[16,128]{1,0:T(8,128)(2,1)} %bitcast.261, bf16[32,3072]{1,0:T(8,128)(2,1)} %convert_element_type.146.refs_1_, ...), custom_call_target="tpu_custom_call" | custom-call | tf_op jit(solution)/shard_map/gather_all/pallas_call | solution.py:155
  138.2 4.6 fusion.72
  148.8 8.1 %fusion.123 = f32[256,4096]{1,0:T(8,128)} fusion(bf16[256,1024]{1,0:T(8,128)(2,1)S(1)} %bitcast.257, bf16[4096,1024]{1,0:T(8,128)(2,1)} %bitcast.265), kind=kOutput, calls=%fused_computation.215 | convolution fusion | flops 2147483648 | bytes 13107200 | tf_op jit(solution)/shard_map/dot_general | solution.py:417
  157.0 43.6 %all-gather.3.cloned.1.call-done = bf16[2,1024,16,64]{1,0,3,2:T(2,128)(2,1)} async-done(((bf16[2,128,16,64]{1,0,3,2:T(2,128)(2,1)}), bf16[2,1024,16,64]{1,0,3,2:T(2,128)(2,1)}) %all-gather.3.cloned.1.call-update) | async-done | bytes 4194320 | tf_op jit(solution)/shard_map/all_gather | solution.py:542
  200.6 5.5 copy.68
  206.0 48.3 %all-gather.5.cloned.1.call-done = bf16[2,1024,16,64]{1,0,3,2:T(2,128)(2,1)} async-done(((bf16[2,128,16,64]{1,0,3,2:T(2,128)(2,1)}), bf16[2,1024,16,64]{1,0,3,2:T(2,128)(2,1)}) %all-gather.5.cloned.1.call-update) | async-done | bytes 4194320 | tf_op jit(solution)/shard_map/all_gather | solution.py:541
  254.3 5.5 copy.70
  259.9 30.4 %while.24 = (s32[]{:T(128)}, bf16[2,128,16,64]{1,3,2,0:T(8,128)(2,1)S(1)}, bf16[2,1024,16,64]{1,3,2,0:T(8,128)(2,1)}, s32[1024]{0:T(1024)S(1)}, s32[128]{0:T(128...) while((s32[]{:T(128)}, ...), condition=%wide.region_7.8_spmd, body=%wide.region_4.7_spmd.sunk | while | flops 553912320 | bytes 55603856 | solution.py:557
  264.4 5.7 fusion.165
  270.0 5.1 fusion.166
  279.5 5.7 fusion.165
  285.2 5.1 fusion.166
  294.1 10.0 %convert_reduce_fusion = (f32[4096]{0:T(1024)}, bf16[256,4096]{1,0:T(8,128)(2,1)S(1)}, f32[256,4096]{1,0:T(8,128)}) fusion(f32[256,4096]{1,0:T(8,128)S(1)} %copy-done.59, f32[4096]{0:T(1024)S(1)} %slice_bitcast_fusion, bf16[1024,4096]{1,0:T(8,128)(2,1)} %bitcast.269, f32[256,1024]{1,0:T(8,128)S(1)} %get-tuple-element.309, f32[1024]{0:T(1024)S(1)} %add.275, ...), kind=kOutput, calls=%fused_computation.80 | convolution fusion | flops 2172907520 | bytes 19965952 | tf_op jit(solution)/shard_map/dot_general | solution.py:562
  304.1 3.2 multiply_reduce_fusion.1
  312.0 45.6 %while.25 = (s32[]{:T(128)}, bf16[2,128,16,64]{1,3,2,0:T(8,128)(2,1)S(1)}, f32[2,1024,16,64]{1,3,2,0:T(8,128)}, f32[2,1024,16,64]{1,3,2,0:T(8,128)}, bf16[2,1024...) while((s32[]{:T(128)}, ...), condition=%wide.region_16.17_spmd, body=%wide.region_12.16_spmd.sunk | while | flops 1375076352 | bytes 171769584 | solution.py:610
  316.6 3.7 fusion.176
  320.3 3.2 multiply_reduce_fusion.8
  331.7 3.2 copy-done.9
  339.2 3.7 fusion.176
  343.0 3.2 multiply_reduce_fusion.8
  354.4 3.2 copy-done.9
  357.6 11.7 %reduce-scatter.5.cloned.1.call-start = ((), (), s32[]{:S(2)}) async-start(), calls=%async_computation.5 | async-start | bytes 9437184 | tf_op jit(solution)/shard_map/reduce_scatter | solution.py:615
  376.5 3.1 convolution_convert_fusion.3
  379.7 5.7 convolution_convert_fusion
  385.4 5.3 convolution_convert_fusion.1
  390.7 3.8 fusion.74
  394.5 52.9 %reduce-scatter.3.cloned.1.call-done = f32[2,128,16,64]{1,3,2,0:T(8,128)} async-done(((f32[2,1024,16,64]{1,3,2,0:T(8,128)}), f32[2,128,16,64]{1,3,2,0:T(8,128)}) %reduce-scatter.3.cloned.1.call-update) | async-done | bytes 1048592 | tf_op jit(solution)/shard_map/reduce_scatter | solution.py:614
  450.0 87.5 %reduce-scatter.5.cloned.1.call-done = f32[2,128,16,64]{1,3,2,0:T(8,128)} async-done(((f32[2,1024,16,64]{1,3,2,0:T(8,128)}), f32[2,128,16,64]{1,3,2,0:T(8,128)}) %reduce-scatter.5.cloned.1.call-update) | async-done | bytes 1048592 | tf_op jit(solution)/shard_map/reduce_scatter | solution.py:615
  540.8 4.9 fusion.107
  547.9 4.5 convolution_convert_fusion.2
  553.7 144.9 %scatter_all.1 = (f32[128,1024]{1,0:T(8,128)}, f32[32,4096]{1,0:T(8,128)}, f32[32,1024]{1,0:T(8,128)}, f32[32,3072]{1,0:T(8,128)}, f32[16,128]{1,0:T(8,128)}, /*index=5*/f32[8,128]{1,0:T(8,128)}) custom-call(bf16[4,4,2,128,1024]{4,3,2,1,0:T(8,128)(2,1)} %bitcast.241, bf16[4,4,2,32,4096]{4,3,2,1,0:T(8,128)(2,1)} %bitcast.238, ...), custom_call_target="tpu_custom_call" | custom-call | tf_op jit(solution)/shard_map/scatter_all/pallas_call | solution.py:384
  703.5 3.1 multiply_subtract_fusion.2
  (271 shorter events, 89.3 us)
Async XLA Ops:
  7.2 129.0 %copy-start.3 = (bf16[2,128,1024]{2,1,0:T(8,128)(2,1)S(1)}, bf16[2,128,1024]{2,1,0:T(8,128)(2,1)}, u32[]{:S(2)}) copy-start(bf16[2,128,1024]{2,1,0:T(8,128)(2,1)} %param.28) | copy-start | bytes 1572868
  7.2 193.4 %all-gather.3.cloned.1.call-start = ((), (), s32[]{:S(2)}) async-start(), calls=%async_computation.2 | async-start | bytes 4718592 | tf_op jit(solution)/shard_map/all_gather | solution.py:542
  144.2 110.1 %all-gather.5.cloned.1.call-start = ((), (), s32[]{:S(2)}) async-start(), calls=%async_computation.3 | async-start | bytes 4718592 | tf_op jit(solution)/shard_map/all_gather | solution.py:541
  145.4 301.9 %reduce-scatter.3.cloned.1.call-start = ((), (), s32[]{:S(2)}) async-start(), calls=%async_computation.4 | async-start | bytes 9437184 | tf_op jit(solution)/shard_map/reduce_scatter | solution.py:614
  147.7 146.4 %copy-start.30 = (f32[1024]{0:T(1024)}, f32[1024]{0:T(1024)S(1)}, u32[]{:S(2)}) copy-start(f32[1024]{0:T(1024)S(1)} %add.275) | copy-start | bytes 12292
  147.7 159.6 %copy-start.28 = (f32[1024]{0:T(1024)}, f32[1024]{0:T(1024)S(1)}, u32[]{:S(2)}) copy-start(f32[1024]{0:T(1024)S(1)} %mul.503) | copy-start | bytes 12292
  148.8 158.9 %copy-start.5 = (f32[2,128,1024]{2,1,0:T(8,128)}, f32[2,128,1024]{2,1,0:T(8,128)S(1)}, u32[]{:S(2)}) copy-start(f32[2,128,1024]{2,1,0:T(8,128)S(1)} %get-tuple-element.297) | copy-start | bytes 3145732
  290.9 13.2 %copy-start.10 = (bf16[2,128,16,64]{1,0,3,2:T(2,128)(2,1)}, bf16[2,128,16,64]{1,0,3,2:T(2,128)(2,1)S(1)}, u32[]{:S(2)}) copy-start(bf16[2,128,16,64]{1,0,3,2:T(2,128)(2,1)S(1)} %copy.71) | copy-start | bytes 1572868
  290.9 13.2 %slice-start.4 = ((s8[8388608]{0:T(1024)(128)(4,1)}), s8[4194304]{0:T(1024)(128)(4,1)S(1)}, s32[]{:S(2)}) async-start(s8[8388608]{0:T(1024)(128)(4,1)} %bitcast.270), calls=%async_computation.10 | async-start | bytes 8388608
  293.8 13.6 %copy-start.1 = (f32[256,1024]{1,0:T(8,128)}, f32[256,1024]{1,0:T(8,128)S(1)}, u32[]{:S(2)}) copy-start(f32[256,1024]{1,0:T(8,128)S(1)} %get-tuple-element.309) | copy-start | bytes 3145732
  293.8 13.5 %copy-start.37 = (f32[256]{0:T(256)}, f32[256]{0:T(256)S(1)}, u32[]{:S(2)}) copy-start(f32[256]{0:T(256)S(1)} %broadcast_multiply_fusion) | copy-start | bytes 3076
  294.1 13.3 %copy-start.40 = (f32[256]{0:T(256)}, f32[256]{0:T(256)S(1)}, u32[]{:S(2)}) copy-start(f32[256]{0:T(256)S(1)} %fusion.100) | copy-start | bytes 3076
  357.6 179.9 %reduce-scatter.5.cloned.1.call-start = ((), (), s32[]{:S(2)}) async-start(), calls=%async_computation.5 | async-start | bytes 9437184 | tf_op jit(solution)/shard_map/reduce_scatter | solution.py:615
  369.4 10.1 %copy-start.2 = (f32[256,1024]{1,0:T(8,128)S(1)}, f32[256,1024]{1,0:T(8,128)}, u32[]{:S(2)}) copy-start(f32[256,1024]{1,0:T(8,128)} %copy-done.1) | copy-start | bytes 3145732
  369.4 10.1 %copy-start.29 = (f32[1024]{0:T(1024)S(1)}, f32[1024]{0:T(1024)}, u32[]{:S(2)}) copy-start(f32[1024]{0:T(1024)} %copy-done.28) | copy-start | bytes 12292
  369.5 10.1 %copy-start.31 = (f32[1024]{0:T(1024)S(1)}, f32[1024]{0:T(1024)}, u32[]{:S(2)}) copy-start(f32[1024]{0:T(1024)} %copy-done.30) | copy-start | bytes 12292
  369.5 10.1 %copy-start.38 = (f32[256]{0:T(256)S(1)}, f32[256]{0:T(256)}, u32[]{:S(2)}) copy-start(f32[256]{0:T(256)} %copy-done.37) | copy-start | bytes 3076
  379.6 11.0 %slice-start.2 = ((s8[8388608]{0:T(1024)(128)(4,1)}), s8[4194304]{0:T(1024)(128)(4,1)S(1)}, s32[]{:S(2)}) async-start(s8[8388608]{0:T(1024)(128)(4,1)} %bitcast.266), calls=%async_computation.8 | async-start | bytes 8388608
  394.4 145.1 %copy-start.13 = (bf16[256,3072]{0,1:T(8,128)(2,1)S(1)}, bf16[256,3072]{0,1:T(8,128)(2,1)}, u32[]{:S(2)}) copy-start(bf16[256,3072]{0,1:T(8,128)(2,1)} %bitcast_dynamic-update-slice_fusion.4) | copy-start | bytes 4718596
  394.4 146.3 %copy-start.4 = (bf16[2,128,1024]{2,1,0:T(8,128)(2,1)S(1)}, bf16[2,128,1024]{2,1,0:T(8,128)(2,1)}, u32[]{:S(2)}) copy-start(bf16[2,128,1024]{2,1,0:T(8,128)(2,1)} %param.28) | copy-start | bytes 1572868
  394.4 146.3 %copy-start.33 = (f32[1024]{0:T(1024)S(1)}, f32[1024]{0:T(1024)}, u32[]{:S(2)}) copy-start(f32[1024]{0:T(1024)} %copy-done.32) | copy-start | bytes 12292
  394.4 146.3 %copy-start.46 = (f32[256]{0:T(256)S(1)}, f32[256]{0:T(256)}, u32[]{:S(2)}) copy-start(f32[256]{0:T(256)} %get-tuple-element.300) | copy-start | bytes 3076
  553.7 147.9 %copy-start.57 = (f32[128]{0:T(128)S(1)}, f32[128]{0:T(128)}, u32[]{:S(2)}) copy-start(f32[128]{0:T(128)} %param.39) | copy-start | bytes 1540
  553.7 147.9 %copy-start.58 = (f32[128]{0:T(128)S(1)}, f32[128]{0:T(128)}, u32[]{:S(2)}) copy-start(f32[128]{0:T(128)} %param.51) | copy-start | bytes 1540
  553.7 149.8 %copy-start.20 = (f32[32,3072]{1,0:T(8,128)S(1)}, f32[32,3072]{1,0:T(8,128)}, u32[]{:S(2)}) copy-start(f32[32,3072]{1,0:T(8,128)} %param.34) | copy-start | bytes 1179652
  553.7 155.4 %copy-start.17 = (f32[32,4096]{1,0:T(8,128)S(1)}, f32[32,4096]{1,0:T(8,128)}, u32[]{:S(2)}) copy-start(f32[32,4096]{1,0:T(8,128)} %param.36) | copy-start | bytes 1572868
  553.7 155.4 %copy-start.21 = (f32[32,4096]{1,0:T(8,128)S(1)}, f32[32,4096]{1,0:T(8,128)}, u32[]{:S(2)}) copy-start(f32[32,4096]{1,0:T(8,128)} %param.48) | copy-start | bytes 1572868
  553.7 155.4 %copy-start.22 = (f32[32,4096]{1,0:T(8,128)S(1)}, f32[32,4096]{1,0:T(8,128)}, u32[]{:S(2)}) copy-start(f32[32,4096]{1,0:T(8,128)} %param.42) | copy-start | bytes 1572868
  698.7 13.5 %copy-start.18 = (f32[128,1024]{1,0:T(8,128)S(1)}, f32[128,1024]{1,0:T(8,128)}, u32[]{:S(2)}) copy-start(f32[128,1024]{1,0:T(8,128)} %param.37) | copy-start | bytes 1572868
  698.7 13.5 %copy-start.23 = (f32[128,1024]{1,0:T(8,128)S(1)}, f32[128,1024]{1,0:T(8,128)}, u32[]{:S(2)}) copy-start(f32[128,1024]{1,0:T(8,128)} %param.49) | copy-start | bytes 1572868
  698.7 13.5 %copy-start.24 = (f32[128,1024]{1,0:T(8,128)S(1)}, f32[128,1024]{1,0:T(8,128)}, u32[]{:S(2)}) copy-start(f32[128,1024]{1,0:T(8,128)} %param.43) | copy-start | bytes 1572868
  701.6 10.6 %copy-start.25 = (f32[128,1024]{1,0:T(8,128)S(1)}, f32[128,1024]{1,0:T(8,128)}, u32[]{:S(2)}) copy-start(f32[128,1024]{1,0:T(8,128)} %get-tuple-element.146) | copy-start | bytes 1572868
  (44 other events, 192.1 us)
Sparse Core Ops, SparseCore 0:
  144.3 56.1 all-gather.2
  202.7 51.5 all-gather.4
  357.7 89.5 reduce-scatter.2
  449.5 87.9 reduce-scatter.4

commit v2 on v1

--- a/solution.py
+++ b/solution.py
@@ -1,5 +1,4 @@
 import functools
-import math
 
 import jax
 import jax.numpy as jnp
@@ -394,6 +393,289 @@
     )(*grads)
 
 
+class Heads:
+    def __init__(self, seq_size, pairs, seqs):
+        self.seq_size, self.pairs = seq_size, pairs
+        self.units = seqs * pairs // seq_size
+        self.dp = lax.axis_index("dp")
+        self.seq = lax.axis_index("seq")
+        self.peers = [(self.seq + j) % seq_size for j in range(1, seq_size)]
+
+    def share(self, seq):
+        return seq % self.pairs, pl.ds((seq // self.pairs) * self.units, self.units)
+
+    def to_heads(self, rows, units, local_sem, send_sem, recv_sem):
+        copies = []
+        for j, peer in enumerate(self.peers):
+            pair, which = self.share(peer)
+            copies.append(
+                pltpu.make_async_remote_copy(
+                    src_ref=rows.at[:, pair, which],
+                    dst_ref=units.at[:, :, self.seq],
+                    send_sem=send_sem.at[j],
+                    recv_sem=recv_sem.at[j],
+                    device_id=(self.dp, peer),
+                    device_id_type=MESH,
+                )
+            )
+        pair, which = self.share(self.seq)
+        copies.append(
+            pltpu.make_async_copy(rows.at[:, pair, which], units.at[:, :, self.seq], local_sem)
+        )
+        for copy in copies:
+            copy.start()
+        return copies
+
+    def to_rows(self, units, rows, local_sem, send_sem, recv_sem):
+        copies = []
+        pair, which = self.share(self.seq)
+        for j, peer in enumerate(self.peers):
+            copies.append(
+                pltpu.make_async_remote_copy(
+                    src_ref=units.at[:, :, peer],
+                    dst_ref=rows.at[:, pair, which],
+                    send_sem=send_sem.at[j],
+                    recv_sem=recv_sem.at[j],
+                    device_id=(self.dp, peer),
+                    device_id_type=MESH,
+                )
+            )
+        copies.append(
+            pltpu.make_async_copy(units.at[:, :, self.seq], rows.at[:, pair, which], local_sem)
+        )
+        for copy in copies:
+            copy.start()
+        return copies
+
+    def unit_sequence(self, unit):
+        return (self.seq // self.pairs) * self.units + unit
+
+
+def head_lanes(rows, head):
+    lane = lax.broadcasted_iota(jnp.int32, rows.shape, 1)
+    return jnp.where(lane // HD == head, rows, jnp.zeros_like(rows))
+
+
+CHUNK = 256
+
+
+def attend(heads, qkv, key_pos, query_pos, context, stats):
+    units, length = context.shape[0], query_pos.shape[1]
+    tall = qkv.shape[2] * qkv.shape[3]
+    for unit in range(units):
+        keys = qkv[1, unit].reshape(tall, 128)
+        values_t = qkv[2, unit].reshape(tall, 128).T
+        pos = key_pos[heads.unit_sequence(unit)][:, :1]
+
+        def chunk(i, carry, unit=unit, keys=keys, values_t=values_t, pos=pos):
+            where = pl.ds(pl.multiple_of(i * CHUNK, CHUNK), CHUNK)
+            queries = context_rows(qkv.at[0, unit], where) * 0.125
+            allowed = pos <= query_pos[:, where]
+            halves = []
+            for head in range(2):
+                scores = contract_cols(keys, head_lanes(queries, head))
+                scores = jnp.where(allowed, scores, neg_fill)
+                top = jnp.max(scores, axis=0, keepdims=True)
+                exp_scores = jnp.exp(scores - top)
+                total = jnp.sum(exp_scores, axis=0, keepdims=True)
+                weights = (exp_scores * (1.0 / total)).astype(jnp.bfloat16)
+                stats[unit, head, :, where] = top + jnp.log(total)
+                halves.append(
+                    jnp.dot(
+                        values_t[head * HD : (head + 1) * HD],
+                        weights,
+                        preferred_element_type=jnp.float32,
+                    )
+                )
+            rows = jnp.concatenate(halves, axis=0).T.astype(jnp.bfloat16)
+            store_rows(context.at[unit], where, rows)
+            return carry
+
+        lax.fori_loop(0, length // CHUNK, chunk, 0)
+
+
+def context_rows(ref, where):
+    slots = ref.shape[1]
+    some = ref[pl.ds(where.start // slots, CHUNK // slots)]
+    return some.reshape(CHUNK, 128)
+
+
+def store_rows(ref, where, rows):
+    slots = ref.shape[1]
+    ref[pl.ds(where.start // slots, CHUNK // slots)] = rows.reshape(CHUNK // slots, slots, 128)
+
+
+def attend_back(heads, qkv, grad_ctx, key_pos, query_pos, stats, grads, key_sum, value_sum):
+    units, length = grad_ctx.shape[0], query_pos.shape[1]
+    tall = qkv.shape[2] * qkv.shape[3]
+    for unit in range(units):
+        keys = qkv[1, unit].reshape(tall, 128)
+        keys_t = keys.T
+        values = qkv[2, unit].reshape(tall, 128)
+        pos = key_pos[heads.unit_sequence(unit)][:, :1]
+        key_sum[...] = jnp.zeros_like(key_sum)
+        value_sum[...] = jnp.zeros_like(value_sum)
+
+        def chunk(i, carry, unit=unit, keys=keys, keys_t=keys_t, values=values, pos=pos):
+            where = pl.ds(pl.multiple_of(i * CHUNK, CHUNK), CHUNK)
+            queries = context_rows(qkv.at[0, unit], where) * 0.125
+            grad_rows = context_rows(grad_ctx.at[unit], where)
+            allowed = pos <= query_pos[:, where]
+            halves = []
+            for head in range(2):
+                queries_h = head_lanes(queries, head)
+                grad_h = head_lanes(grad_rows, head)
+                scores = jnp.where(allowed, contract_cols(keys, queries_h), neg_fill)
+                weights = jnp.exp(scores - stats[unit, head, :, where])
+                grad_prob = contract_cols(values, grad_h)
+                delta = jnp.sum(weights * grad_prob, axis=0, keepdims=True)
+                grad_score = (weights * (grad_prob - delta)).astype(jnp.bfloat16)
+                value_sum[...] += jnp.dot(
+                    weights.astype(jnp.bfloat16), grad_h, preferred_element_type=jnp.float32
+                )
+                key_sum[...] += jnp.dot(
+                    grad_score, queries_h, preferred_element_type=jnp.float32
+                )
+                halves.append(
+                    jnp.dot(
+                        keys_t[head * HD : (head + 1) * HD],
+                        grad_score,
+                        preferred_element_type=jnp.float32,
+                    )
+                )
+            rows = (jnp.concatenate(halves, axis=0).T * 0.125).astype(jnp.bfloat16)
+            store_rows(grads.at[0, unit], where, rows)
+            return carry
+
+        lax.fori_loop(0, length // CHUNK, chunk, 0)
+        shape = grads.shape[2:]
+        grads[1, unit] = key_sum[...].astype(jnp.bfloat16).reshape(shape)
+        grads[2, unit] = value_sum[...].astype(jnp.bfloat16).reshape(shape)
+
+
+def forward_kernel(
+    seq_size,
+    seqs,
+    rows,
+    key_pos,
+    query_pos,
+    context_rows_out,
+    qkv,
+    stats,
+    context,
+    local_sem,
+    send_sem,
+    recv_sem,
+):
+    heads = Heads(seq_size, rows.shape[1], seqs)
+    greet([(heads.dp, peer) for peer in heads.peers])
+    for copy in heads.to_heads(rows, qkv, local_sem.at[0], send_sem.at[0], recv_sem.at[0]):
+        copy.wait()
+    attend(heads, qkv, key_pos, query_pos, context.at[0], stats)
+    for copy in heads.to_rows(
+        context, context_rows_out, local_sem.at[1], send_sem.at[1], recv_sem.at[1]
+    ):
+        copy.wait()
+
+
+def backward_kernel(
+    seq_size,
+    seqs,
+    rows,
+    qkv,
+    stats,
+    key_pos,
+    query_pos,
+    grad_rows_out,
+    grad_ctx,
+    grads,
+    key_sum,
+    value_sum,
+    local_sem,
+    send_sem,
+    recv_sem,
+):
+    heads = Heads(seq_size, rows.shape[1], seqs)
+    greet([(heads.dp, peer) for peer in heads.peers])
+    for copy in heads.to_heads(rows, grad_ctx, local_sem.at[0], send_sem.at[0], recv_sem.at[0]):
+        copy.wait()
+    attend_back(
+        heads, qkv, grad_ctx.at[0], key_pos, query_pos, stats, grads, key_sum, value_sum
+    )
+    for copy in heads.to_rows(
+        grads, grad_rows_out, local_sem.at[1], send_sem.at[1], recv_sem.at[1]
+    ):
+        copy.wait()
+
+
+def exchange_sems(seq_size):
+    return [
+        pltpu.SemaphoreType.DMA((2,)),
+        pltpu.SemaphoreType.DMA((2, seq_size - 1)),
+        pltpu.SemaphoreType.DMA((2, seq_size - 1)),
+    ]
+
+
+VMEM_SPEC = pl.BlockSpec(memory_space=pltpu.VMEM)
+
+
+def attention_forward(rows, key_pos, query_pos, seq_size):
+    pairs, seqs, slots = rows.shape[1:4]
+    units = seqs * pairs // seq_size
+    shapes = [
+        jax.ShapeDtypeStruct((1,) + rows.shape[1:], rows.dtype),
+        jax.ShapeDtypeStruct((3, units, seq_size, slots, 128), rows.dtype),
+        jax.ShapeDtypeStruct((units, 2, 1, seq_size * slots), jnp.float32),
+    ]
+    return pl.pallas_call(
+        functools.partial(forward_kernel, seq_size, seqs),
+        out_shape=shapes,
+        in_specs=[VMEM_SPEC] * 3,
+        out_specs=[VMEM_SPEC] * 3,
+        scratch_shapes=[pltpu.VMEM((1, units, seq_size, slots, 128), rows.dtype)]
+        + exchange_sems(seq_size),
+        compiler_params=pltpu.CompilerParams(
+            collective_id=2, has_side_effects=True, vmem_limit_bytes=40 << 20
+        ),
+        name="attention_forward",
+    )(rows, key_pos, query_pos)
+
+
+def attention_backward(rows, qkv, stats, key_pos, query_pos, seq_size):
+    pairs, seqs, slots = rows.shape[1:4]
+    units = seqs * pairs // seq_size
+    length = seq_size * slots
+    return pl.pallas_call(
+        functools.partial(backward_kernel, seq_size, seqs),
+        out_shape=jax.ShapeDtypeStruct((3,) + rows.shape[1:], rows.dtype),
+        in_specs=[VMEM_SPEC] * 5,
+        out_specs=VMEM_SPEC,
+        scratch_shapes=[
+            pltpu.VMEM((1, units, seq_size, slots, 128), rows.dtype),
+            pltpu.VMEM((3, units, seq_size, slots, 128), rows.dtype),
+            pltpu.VMEM((length, 128), jnp.float32),
+            pltpu.VMEM((length, 128), jnp.float32),
+        ]
+        + exchange_sems(seq_size),
+        compiler_params=pltpu.CompilerParams(
+            collective_id=3, has_side_effects=True, vmem_limit_bytes=40 << 20
+        ),
+        name="attention_backward",
+    )(rows, qkv, stats, key_pos, query_pos)
+
+
+def contract_rows(left, right):
+    return lax.dot_general(
+        left, right, (((0,), (0,)), ((), ())), preferred_element_type=jnp.float32
+    )
+
+
+def contract_cols(left, right):
+    return lax.dot_general(
+        left, right, (((1,), (1,)), ((), ())), preferred_element_type=jnp.float32
+    )
+
+
 def layer_norm(values, gain_vec, shift_vec):
     centered = values - jnp.mean(values, axis=-1, keepdims=True)
     variance = jnp.mean(centered * centered, axis=-1, keepdims=True)
@@ -405,35 +687,6 @@
     one_hot = (slot_ids[:, None] // block_len == block_ids[None, :]).astype(jnp.int32)
     picked = jnp.sum(one_hot * order_table[None, :], axis=1)
     return picked * block_len + slot_ids % block_len
-
-
-def contract_rows(left, right):
-    return lax.dot_general(
-        left, right, (((0,), (0,)), ((), ())), preferred_element_type=jnp.float32
-    )
-
-
-def contract_cols(left, right):
-    return lax.dot_general(
-        left, right, (((1,), (1,)), ((), ())), preferred_element_type=jnp.float32
-    )
-
-
-def masked_scores(queries, key_block, query_pos, key_pos, length, score_scale):
-    scores = (
-        jnp.einsum("qhd,khd->hqk", queries, key_block, preferred_element_type=jnp.float32)
-        * score_scale
-    )
-    allowed = (key_pos[None, :] <= query_pos[:, None]) & (key_pos[None, :] < length)
-    return jnp.where(allowed[None], scores, neg_fill)
-
-
-def softmax_rows(queries, key_block, query_pos, key_pos, length, score_scale):
-    scores = masked_scores(queries, key_block, query_pos, key_pos, length, score_scale)
-    row_max = jnp.max(scores, axis=-1, keepdims=True)
-    exp_scores = jnp.exp(scores - row_max)
-    row_total = jnp.sum(exp_scores, axis=-1, keepdims=True)
-    return (exp_scores / row_total, row_max + jnp.log(row_total))
 
 
 def pack_small(vec_cols, bias, devices):
@@ -488,7 +741,6 @@
     hidden = w_expand.shape[1]
     total_slots = local_slots * seq_size
     block_len = total_slots // block_order.shape[0]
-    score_scale = 1.0 / math.sqrt(HD)
     token_count = seqs_here * local_slots
     first_slot = lax.axis_index("seq") * local_slots
     local_pos = slot_positions(
@@ -533,29 +785,16 @@
     qkv_rows = (jnp.dot(normed_one, qkv_full, preferred_element_type=wide_type) + bias_cat).astype(
         low_type
     )
-    head_shape = (seqs_here, local_slots, HEADS, HD)
-    query_all = qkv_rows[:, :model_width].reshape(head_shape)
-    key_local = qkv_rows[:, model_width : 2 * model_width].reshape(head_shape)
-    value_local = qkv_rows[:, 2 * model_width :].reshape(head_shape)
-    keys_all, values_all = (
-        lax.all_gather(key_local, "seq", axis=1, tiled=True),
-        lax.all_gather(value_local, "seq", axis=1, tiled=True),
-    )
-
-    def forward_one(packed):
-        queries, key_block, value_block, length = packed
-        softmax_w, row_lse = softmax_rows(
-            queries, key_block, local_pos, key_pos, length, score_scale
-        )
-        return jnp.einsum(
-            "hqk,khd->qhd",
-            softmax_w.astype(low_type),
-            value_block,
-            preferred_element_type=wide_type,
-        )
-
-    context = lax.map(forward_one, (query_all, keys_all, values_all, lengths))
-    context_low = context.reshape(token_count, model_width).astype(low_type)
+    pairs = HEADS // 2
+    row_shape = (seqs_here, local_slots, -1, pairs, 128)
+    qkv_heads = qkv_rows.reshape(row_shape).transpose(2, 3, 0, 1, 4)
+    far = jnp.where(key_pos[None, :] < lengths[:, None], key_pos[None, :], 2**30)
+    key_limits = jnp.broadcast_to(far[:, :, None], (seqs_here, total_slots, 128))
+    query_row = key_pos[None, :]
+    context, qkv_units, row_stats = attention_forward(
+        qkv_heads, key_limits, query_row, seq_size
+    )
+    context_low = context[0].transpose(1, 2, 0, 3).reshape(token_count, model_width)
     attn_rows = jnp.dot(context_low, proj_full, preferred_element_type=wide_type) + bias_proj
     resid = rows_in + attn_rows
     normed_two = layer_norm(resid, gain_two, shift_two).astype(low_type)
@@ -582,44 +821,14 @@
     grad_attn_low = grad_resid.astype(low_type)
     grad_proj = contract_rows(context_low, grad_attn_low)
     grad_bias_proj = jnp.sum(grad_attn_low, axis=0, dtype=wide_type)
-    grad_context = contract_cols(grad_attn_low, proj_full).astype(low_type).reshape(head_shape)
-
-    def backward_one(packed):
-        queries, key_block, value_block, grad_ctx, length = packed
-        softmax_w, row_lse = softmax_rows(
-            queries, key_block, local_pos, key_pos, length, score_scale
-        )
-        grad_prob = jnp.einsum(
-            "qhd,khd->hqk", grad_ctx, value_block, preferred_element_type=wide_type
-        )
-        delta = jnp.sum(softmax_w * grad_prob, axis=-1, keepdims=True)
-        grad_score = (softmax_w * (grad_prob - delta)).astype(low_type)
-        grad_query = (
-            jnp.einsum("hqk,khd->qhd", grad_score, key_block, preferred_element_type=wide_type)
-            * score_scale
-        )
-        key_terms = (
-            jnp.einsum("hqk,qhd->khd", grad_score, queries, preferred_element_type=wide_type)
-            * score_scale
-        )
-        value_terms = jnp.einsum(
-            "hqk,qhd->khd", softmax_w.astype(low_type), grad_ctx, preferred_element_type=wide_type
-        )
-        return (grad_query, key_terms, value_terms)
-
-    grad_query, key_terms, value_terms = lax.map(
-        backward_one, (query_all, keys_all, values_all, grad_context, lengths)
-    )
-    key_sums, value_sums = (
-        lax.psum_scatter(key_terms, "seq", scatter_dimension=1, tiled=True),
-        lax.psum_scatter(value_terms, "seq", scatter_dimension=1, tiled=True),
-    )
-    grad_q_low = grad_query.reshape(token_count, model_width).astype(low_type)
-    grad_v_low = value_sums.reshape(token_count, model_width).astype(low_type)
-    grad_qkv_rows = jnp.concatenate(
-        [grad_q_low, key_sums.reshape(token_count, model_width).astype(low_type), grad_v_low],
-        axis=1,
-    )
+    grad_context = contract_cols(grad_attn_low, proj_full).astype(low_type)
+    grad_context = grad_context.reshape(row_shape).transpose(2, 3, 0, 1, 4)
+    grad_heads = attention_backward(
+        grad_context, qkv_units, row_stats, key_limits, query_row, seq_size
+    )
+    grad_qkv_rows = grad_heads.transpose(2, 3, 0, 1, 4).reshape(token_count, 3 * model_width)
+    grad_q_low = grad_qkv_rows[:, :model_width]
+    grad_v_low = grad_qkv_rows[:, 2 * model_width :]
     grad_qkv_w = contract_rows(normed_one, grad_qkv_rows)
     grad_bias_query = jnp.sum(grad_q_low, axis=0, dtype=wide_type)
     grad_bias_value = jnp.sum(grad_v_low, axis=0, dtype=wide_type)

time: 730 us -> 510 us (0.70)
  waiting for transfers between devices: 232 us -> 0 us
  Pallas kernels: 263 us -> 399 us
  matrix products: 95.6 us -> 54.3 us
  local copies, waits for them, and re-layouts: 42.7 us -> 14.9 us
  other arithmetic: 59.2 us -> 32.6 us
  between operations: 17.5 us -> 4.1 us
  starting transfers between devices: 12.3 us -> 0 us
    reduce_scatter x2 -> x0, waiting for transfers between devices: 140 us -> none  [the longest x1 87.5 us: per_device(): lax.psum_scatter(value_terms, 'seq', scatter_dimension=1, tiled=True)]
    pallas_call x0 -> x2, Pallas kernels: none -> 123 us  [the longest x1 66.3 us: attention_forward(): pl.pallas_call(functools.partial(forward_kernel, seq_size, seqs), out_sha...]
    all_gather x2 -> x0, waiting for transfers between devices: 91.8 us -> none  [the longest x1 48.3 us: per_device(): lax.all_gather(key_local, 'seq', axis=1, tiled=True)]
    dot_general x14 -> x0, matrix products: 38.9 us -> none  [the longest x4 11.5 us: masked_scores(): jnp.einsum('qhd,khd->hqk', queries, key_block, preferred_element_type=jnp...]
    while x24 -> x0, local copies, waits for them, and re-layouts: 22 us -> none  [the longest x3 11.8 us: per_device(): context = lax.map(forward_one, (query_all, keys_all, values_all, lengths))]
    sub x4 -> x0, other arithmetic: 18.8 us -> none  [softmax_rows(): exp_scores = jnp.exp(scores - row_max)]
    pallas_call x1, Pallas kernels: 145 us -> 158 us  [scatter_all(): pl.pallas_call(functools.partial(scatter_kernel, dp_size, seq_size, count...]
    reduce_scatter x2 -> x0, starting transfers between devices: 12.2 us -> none  [the longest x1 11.7 us: per_device(): lax.psum_scatter(value_terms, 'seq', scatter_dimension=1, tiled=True)]
  transfers between devices with their start and end apart: 4 -> 0, of which waited for: 4 -> 0; matrix products, arithmetic and copies ran while one was open for 6% -> 0% of each run, Pallas kernels for 0% -> 0%
where the time goes in v2:
time: 510 us; the launch traced here: 505 us
  Pallas kernels  399 us (78%)
  matrix products  54.3 us (11%)
  other arithmetic  32.6 us (6%)
  local copies, waits for them, and re-layouts  14.9 us (3%)
    pallas_call x1, Pallas kernels, scatter_all(): pl.pallas_call(functools.partial(scatter_kernel, dp_size, seq_size, count...  158 us
    pallas_call x1, Pallas kernels, gather_all(): pl.pallas_call(functools.partial(gather_kernel, dp_size, seq_size, count)...  118 us
    pallas_call x1, Pallas kernels, attention_forward(): pl.pallas_call(functools.partial(forward_kernel, seq_size, seqs), out_sha...  66.3 us
    pallas_call x1, Pallas kernels, attention_backward(): pl.pallas_call(functools.partial(backward_kernel, seq_size, seqs), out_sh...  56.5 us
    dot_general x4, matrix products, contract_rows(): lax.dot_general(left, right, (((0,), (0,)), ((), ())), preferred_element_...  17.6 us
    dot_general x4, matrix products, contract_cols(): lax.dot_general(left, right, (((1,), (1,)), ((), ())), preferred_element_...  16.1 us
    sub x6, other arithmetic, per_device(): renewed.append(masters[group_id] - learn_rates[group_id] * update)  13.8 us
    dot_general x1, matrix products, per_device(): jnp.dot(normed_two, expand_full, preferred_element_type=wide_type)  10.4 us

profile of v2, /device:TPU:0, one launch (start us, length us, event | category | flops | bytes accessed | tf_op | source)
XLA Modules:
  0.0 504.7 jit_solution(16516551725972515296)
XLA Ops:
  2.8 1.7 convert_element_type.108.refs_1_
  4.5 1.5 convert_element_type.109.refs_2_
  6.0 1.8 convert_element_type.110.refs_3_
  7.8 1.8 convert_element_type.111.refs_4_
  9.6 118.0 %gather_all.1 = (bf16[4,4,2,16,128]{4,3,2,1,0:T(8,128)(2,1)}, bf16[4,4,2,32,3072]{4,3,2,1,0:T(8,128)(2,1)}, bf16[4,4,2,32,1024]{4,3,2,1,0:T(8,128)(2,1)}, bf16[4...) custom-call(bf16[16,128]{1,0:T(8,128)(2,1)} %bitcast.156, bf16[32,3072]{1,0:T(8,128)(2,1)} %convert_element_type.108.refs_1_, ...), custom_call_target="tpu_custom_call" | custom-call | tf_op jit(solution)/shard_map/gather_all/pallas_call | solution.py:154
  130.1 4.8 fusion.8
  136.2 66.3 %attention_forward.1 = (bf16[1,8,2,128,128]{4,3,2,1,0:T(8,128)(2,1)S(1)}, bf16[3,2,8,128,128]{4,3,2,1,0:T(8,128)(2,1)S(1)}, f32[2,2,1,1024]{3,2,1,0:T(1,128)S(1)}) custom-call(bf16[3,8,2,128,128]{4,3,2,1,0:T(8,128)(2,1)S(1)} %bitcast.133, s32[2,1024,128]{2,1,0:T(8,128)S(1)} %broadcast_in_dim.24.key_pos, s32[1,1024]{1,0:T(1,128)S(1)} %fusion.32.query_pos), custom_call_target="tpu_custom_call" | custom-call | tf_op jit(solution)/shard_map/attention_forward/pallas_call | solution.py:630
  203.6 1.7 fusion.57
  205.6 2.2 fusion.18
  207.8 7.8 %fusion.58 = f32[256,4096]{1,0:T(8,128)} fusion(bf16[256,1024]{1,0:T(8,128)(2,1)S(1)} %bitcast.152, bf16[4096,1024]{1,0:T(8,128)(2,1)} %bitcast.165), kind=kOutput, calls=%fused_computation.149 | convolution fusion | flops 2147483648 | bytes 13107200 | tf_op jit(solution)/shard_map/dot_general | solution.py:674
  215.7 1.6 multiply_reduce_fusion.4
  217.4 10.4 %convert_reduce_fusion = (f32[4096]{0:T(1024)S(1)}, bf16[256,4096]{1,0:T(8,128)(2,1)S(1)}, f32[256,4096]{1,0:T(8,128)S(1)}) fusion(f32[256,4096]{1,0:T(8,128)} %fusion.58, f32[4096]{0:T(1024)S(1)} %slice_bitcast_fusion, bf16[1024,4096]{1,0:T(8,128)(2,1)} %bitcast.161, f32[256,1024]{1,0:T(8,128)} %get-tuple-element.106, f32[1024]{0:T(1024)S(1)} %add.280, ...), kind=kOutput, calls=%fused_computation.13 | convolution fusion | flops 2172907520 | bytes 19965952 | tf_op jit(solution)/shard_map/dot_general | solution.py:801
  227.8 3.8 fusion.10
  232.6 2.6 multiply_reduce_fusion
  235.9 1.4 copy-done.33
  238.2 56.5 %attention_backward.1 = bf16[3,8,2,128,128]{4,3,2,1,0:T(8,128)(2,1)S(1)} custom-call(bf16[1,8,2,128,128]{4,3,2,1,0:T(8,128)(2,1)S(1)} %bitcast.135, bf16[3,2,8,128,128]{4,3,2,1,0:T(8,128)(2,1)S(1)} %get-tuple-element.41.qkv, f32[2,2,1,1024]{3,2,1,0:T(1,128)S(1)} %get-tuple-element.42.stats, s32[2,1024,128]{2,1,0:T(8,128)S(1)} %broadcast_in_dim.24.key_pos, ...), custom_call_target="tpu_custom_call" | custom-call | tf_op jit(solution)/shard_map/attention_backward/pallas_call | solution.py:648
  294.8 2.2 copy.52
  296.9 2.9 reshape.483
  299.9 4.9 fusion.45
  305.4 1.5 add_add_fusion.2
  307.4 5.3 %convolution_convert_fusion.1 = bf16[4096,1024]{1,0:T(8,128)(2,1)} fusion(bf16[256,1024]{1,0:T(8,128)(2,1)S(1)} %bitcast_convert_fusion, f32[256,4096]{1,0:T(8,128)S(1)} %copy-done.35), kind=kOutput, calls=%fused_computation.1 | convolution fusion | flops 2161115136 | bytes 13107200 | tf_op jit(solution)/shard_map/dot_general | solution.py:668
  312.7 5.8 %convolution_convert_fusion = bf16[1024,4096]{1,0:T(8,128)(2,1)} fusion(bf16[256,4096]{1,0:T(8,128)(2,1)S(1)} %copy-done.10, f32[256,1024]{1,0:T(8,128)S(1)} %copy-done.4, f32[1024]{0:T(1024)S(1)} %add.280, f32[1024]{0:T(1024)S(1)} %mul.489, f32[256]{0:T(256)S(1)} %fusion.38, f32[256]{0:T(256)S(1)} %broadcast_multiply_fusion.1), kind=kOutput, calls=%fused_computation | convolution fusion | flops 2152988672 | bytes 11544576 | tf_op jit(solution)/shard_map/dot_general | solution.py:668
  318.4 2.1 convolution_convert_fusion.3
  320.5 4.5 convolution_convert_fusion.2
  327.0 158.0 %scatter_all.1 = (f32[128,1024]{1,0:T(8,128)}, f32[32,4096]{1,0:T(8,128)}, f32[32,1024]{1,0:T(8,128)}, f32[32,3072]{1,0:T(8,128)}, f32[16,128]{1,0:T(8,128)}, /*index=5*/f32[8,128]{1,0:T(8,128)}) custom-call(bf16[4,4,2,128,1024]{4,3,2,1,0:T(8,128)(2,1)} %bitcast.140, bf16[4,4,2,32,4096]{4,3,2,1,0:T(8,128)(2,1)} %bitcast.137, ...), custom_call_target="tpu_custom_call" | custom-call | tf_op jit(solution)/shard_map/scatter_all/pallas_call | solution.py:383
  485.1 1.4 reduce_sum.209
  488.6 3.1 multiply_subtract_fusion.2
  491.8 2.6 multiply_subtract_fusion.3
  494.4 3.1 multiply_subtract_fusion.1
  497.5 2.1 multiply_subtract_fusion
  500.3 1.2 multiply_subtract_fusion.4
  501.5 1.8 multiply_subtract_fusion.5
  (147 shorter events, 14.5 us)
Async XLA Ops:
  0.7 128.7 %copy-start.2 = (bf16[2,128,1024]{2,1,0:T(8,128)(2,1)S(1)}, bf16[2,128,1024]{2,1,0:T(8,128)(2,1)}, u32[]{:S(2)}) copy-start(bf16[2,128,1024]{2,1,0:T(8,128)(2,1)} %param.24) | copy-start | bytes 1572868
  130.1 4.8 copy-start.7
  135.3 68.4 %copy-start.32 = (bf16[4,4,2,32,1024]{4,3,2,1,0:T(8,128)(2,1)S(1)}, bf16[4,4,2,32,1024]{4,3,2,1,0:T(8,128)(2,1)}, u32[]{:S(2)}) copy-start(bf16[4,4,2,32,1024]{4,3,2,1,0:T(8,128)(2,1)} %get-tuple-element.38) | copy-start | bytes 6291460
  215.7 12.1 %slice-start.2 = ((s8[8388608]{0:T(1024)(128)(4,1)}), s8[4194304]{0:T(1024)(128)(4,1)S(1)}, s32[]{:S(2)}) async-start(s8[8388608]{0:T(1024)(128)(4,1)} %bitcast.166), calls=%async_computation.2 | async-start | bytes 8388608
  217.4 10.4 %copy-start.3 = (f32[256,1024]{1,0:T(8,128)S(1)}, f32[256,1024]{1,0:T(8,128)}, u32[]{:S(2)}) copy-start(f32[256,1024]{1,0:T(8,128)} %get-tuple-element.106) | copy-start | bytes 3145732
  217.4 10.4 %slice-start.3 = ((s8[8388608]{0:T(1024)(128)(4,1)}), s8[4194304]{0:T(1024)(128)(4,1)S(1)}, s32[]{:S(2)}) async-start(s8[8388608]{0:T(1024)(128)(4,1)} %bitcast.166), calls=%async_computation.3 | async-start | bytes 8388608
  217.4 14.2 %slice-start = ((s8[8388608]{0:T(1024)(128)(4,1)}), s8[4194304]{0:T(1024)(128)(4,1)S(1)}, s32[]{:S(2)}) async-start(s8[8388608]{0:T(1024)(128)(4,1)} %bitcast.162), calls=%async_computation | async-start | bytes 8388608
  227.8 3.9 copy-start.34
  227.8 3.8 copy-start.9
  227.8 4.7 slice-start.1
  299.9 5.5 %copy-start.1 = (f32[2,128,1024]{2,1,0:T(8,128)S(1)}, f32[2,128,1024]{2,1,0:T(8,128)}, u32[]{:S(2)}) copy-start(f32[2,128,1024]{2,1,0:T(8,128)} %get-tuple-element.92) | copy-start | bytes 3145732
  299.9 5.5 %copy-start.6 = (f32[256,1024]{1,0:T(8,128)S(1)}, f32[256,1024]{1,0:T(8,128)}, u32[]{:S(2)}) copy-start(f32[256,1024]{1,0:T(8,128)} %copy-done.5) | copy-start | bytes 3145732
  307.4 5.3 %copy-start.4 = (f32[256,1024]{1,0:T(8,128)S(1)}, f32[256,1024]{1,0:T(8,128)}, u32[]{:S(2)}) copy-start(f32[256,1024]{1,0:T(8,128)} %get-tuple-element.106) | copy-start | bytes 3145732
  307.4 5.3 %copy-start.10 = (bf16[256,4096]{1,0:T(8,128)(2,1)S(1)}, bf16[256,4096]{1,0:T(8,128)(2,1)}, u32[]{:S(2)}) copy-start(bf16[256,4096]{1,0:T(8,128)(2,1)} %copy-done.9) | copy-start | bytes 6291460
  312.6 5.8 %copy-start.14 = (bf16[256,1024]{1,0:T(8,128)(2,1)S(1)}, bf16[256,1024]{1,0:T(8,128)(2,1)}, u32[]{:S(2)}) copy-start(bf16[256,1024]{1,0:T(8,128)(2,1)} %copy-done.13) | copy-start | bytes 1572868
  312.6 5.8 %copy-start.16 = (bf16[2,128,8,128]{3,2,1,0:T(8,128)(2,1)S(1)}, bf16[2,128,8,128]{3,2,1,0:T(8,128)(2,1)}, u32[]{:S(2)}) copy-start(bf16[2,128,8,128]{3,2,1,0:T(8,128)(2,1)} %copy-done.15) | copy-start | bytes 1572868
  312.6 7.9 %copy-start.8 = (bf16[2,128,1024]{2,1,0:T(8,128)(2,1)S(1)}, bf16[2,128,1024]{2,1,0:T(8,128)(2,1)}, u32[]{:S(2)}) copy-start(bf16[2,128,1024]{2,1,0:T(8,128)(2,1)} %copy-done.7) | copy-start | bytes 1572868
  327.0 160.9 %copy-start.23 = (f32[6]{0:T(128)S(1)}, f32[6]{0:T(128)}, u32[]{:S(2)}) copy-start(f32[6]{0:T(128)} %param.29) | copy-start | bytes 76
  327.0 161.6 %copy-start.17 = (f32[32,3072]{1,0:T(8,128)S(1)}, f32[32,3072]{1,0:T(8,128)}, u32[]{:S(2)}) copy-start(f32[32,3072]{1,0:T(8,128)} %param.30) | copy-start | bytes 1179652
  327.0 167.4 %copy-start.11 = (f32[32,4096]{1,0:T(8,128)S(1)}, f32[32,4096]{1,0:T(8,128)}, u32[]{:S(2)}) copy-start(f32[32,4096]{1,0:T(8,128)} %param.32) | copy-start | bytes 1572868
  327.0 167.4 %copy-start.18 = (f32[32,4096]{1,0:T(8,128)S(1)}, f32[32,4096]{1,0:T(8,128)}, u32[]{:S(2)}) copy-start(f32[32,4096]{1,0:T(8,128)} %param.44) | copy-start | bytes 1572868
  327.0 167.4 %copy-start.19 = (f32[32,4096]{1,0:T(8,128)S(1)}, f32[32,4096]{1,0:T(8,128)}, u32[]{:S(2)}) copy-start(f32[32,4096]{1,0:T(8,128)} %param.38) | copy-start | bytes 1572868
  485.0 12.4 %copy-start.12 = (f32[128,1024]{1,0:T(8,128)S(1)}, f32[128,1024]{1,0:T(8,128)}, u32[]{:S(2)}) copy-start(f32[128,1024]{1,0:T(8,128)} %param.33) | copy-start | bytes 1572868
  485.1 12.4 %copy-start.20 = (f32[128,1024]{1,0:T(8,128)S(1)}, f32[128,1024]{1,0:T(8,128)}, u32[]{:S(2)}) copy-start(f32[128,1024]{1,0:T(8,128)} %param.45) | copy-start | bytes 1572868
  485.1 12.4 %copy-start.21 = (f32[128,1024]{1,0:T(8,128)S(1)}, f32[128,1024]{1,0:T(8,128)}, u32[]{:S(2)}) copy-start(f32[128,1024]{1,0:T(8,128)} %param.39) | copy-start | bytes 1572868
  488.6 8.9 %copy-start.22 = (f32[128,1024]{1,0:T(8,128)S(1)}, f32[128,1024]{1,0:T(8,128)}, u32[]{:S(2)}) copy-start(f32[128,1024]{1,0:T(8,128)} %get-tuple-element.47) | copy-start | bytes 1572868
  491.8 8.6 %copy-start.24 = (f32[32,8]{0,1:T(8,128)S(1)}, f32[32,8]{0,1:T(8,128)}, u32[]{:S(2)}) copy-start(f32[32,8]{0,1:T(8,128)} %param.34) | copy-start | bytes 3076
  491.8 8.6 %copy-start.25 = (f32[32,8]{0,1:T(8,128)S(1)}, f32[32,8]{0,1:T(8,128)}, u32[]{:S(2)}) copy-start(f32[32,8]{0,1:T(8,128)} %param.46) | copy-start | bytes 3076
  491.8 8.6 %copy-start.26 = (f32[32,8]{0,1:T(8,128)S(1)}, f32[32,8]{0,1:T(8,128)}, u32[]{:S(2)}) copy-start(f32[32,8]{0,1:T(8,128)} %param.40) | copy-start | bytes 3076
  491.8 9.8 %copy-start.29 = (f32[128]{0:T(128)S(1)}, f32[128]{0:T(128)}, u32[]{:S(2)}) copy-start(f32[128]{0:T(128)} %param.35) | copy-start | bytes 1540
  491.8 9.7 %copy-start.30 = (f32[128]{0:T(128)S(1)}, f32[128]{0:T(128)}, u32[]{:S(2)}) copy-start(f32[128]{0:T(128)} %param.47) | copy-start | bytes 1540
  491.8 9.7 %copy-start.31 = (f32[128]{0:T(128)S(1)}, f32[128]{0:T(128)}, u32[]{:S(2)}) copy-start(f32[128]{0:T(128)} %param.41) | copy-start | bytes 1540
  (8 other events, 15.1 us)
